TPU v7x, 512 devices: a whole 4x8x8 slice. The times are simulated.
512 devices in a mesh: plane: 64 (over x, z_lo, y), vert: 8 (over z_hi, core).
Axes of the slice: x: 4, y: 8, z: 8 (z_hi: 4, z_lo: 2; z = z_hi * 2 + z_lo), core: 2. Of those that a mesh axis runs over, the one named last changes fastest.
Arguments:
- source: float32 [128, 512, 512], P('vert', 'plane'), may hold values from -6 to 6
- inv_density: float32 [128, 512, 512], P('vert', 'plane'), may hold values from 0.1 to 10
- pressure: float32 [128, 512, 512], P('vert', 'plane'), may hold values from -6 to 6
Outputs:
- corrected: float32 [128, 512, 512], P('vert', 'plane')
All inputs are finite; a program needn't handle non-finite values.
Results may differ from a plain program's by a relative error of at most 0.00002.
Values sent between devices are 32-bit elements; how exact they have to be, the bound alone decides.
A program may use at most 64 MiB of HBM per device.

v0:
```python
import jax
import jax.numpy as jnp
from jax import lax
from jax.sharding import PartitionSpec as P

LEVELS = 4
COARSE_SWEEPS = 4


RELAX_WEIGHT = 0.8


def extended(array, sides, width):
    for axis, dim in sides:
        peers, length = (lax.axis_size(axis), array.shape[dim])
        up = [(i, (i + 1) % peers) for i in range(peers - 1)]
        down = [(j, i) for i, j in up]
        last = lax.slice_in_dim(array, length - width, length, axis=dim)
        first = lax.slice_in_dim(array, 0, width, axis=dim)
        before = lax.ppermute(last, axis, up)
        after = lax.ppermute(first, axis, down)
        array = jnp.concatenate([before, array, after], axis=dim)
    return array


def neighbours(padded):
    inner = padded.shape
    result = []
    for dimension in range(3):
        for offset in (0, 2):
            window = [slice(1, -1)] * 3
            window[dimension] = slice(offset, offset + inner[dimension] - 2)
            result.append(tuple(window))
    return result


def stencil(field_pad, coef_pad):
    centre = field_pad[1:-1, 1:-1, 1:-1]
    coef_mid = coef_pad[1:-1, 1:-1, 1:-1]
    total = jnp.zeros(centre.shape, jnp.float32)
    for window in neighbours(field_pad):
        total = total + 0.5 * (coef_mid + coef_pad[window]) * (centre - field_pad[window])
    return total


def diagonal(coef_pad):
    coef_mid = coef_pad[1:-1, 1:-1, 1:-1]
    total = jnp.zeros(coef_mid.shape, jnp.float32)
    for window in neighbours(coef_pad):
        total = total + 0.5 * (coef_mid + coef_pad[window])
    return total


def blocks(field):
    a, b, c = field.shape
    return field.reshape(a // 2, 2, b // 2, 2, c // 2, 2).sum(axis=(1, 3, 5))


def prolong(field):
    return jnp.repeat(jnp.repeat(jnp.repeat(field, 2, axis=0), 2, axis=1), 2, axis=2)


def pad_last(field, width):
    return jnp.pad(field, [(0, 0)] * (field.ndim - 1) + [(width, width)])


def faces(field):
    wide = extended(field, (("vert", 0), ("plane", 1)), 1)
    return pad_last(wide, 1)


def relax_many(forcing, coef, extend, column_total):
    coef_pad = extend(coef)
    diag_sum = diagonal(coef_pad)
    guess = RELAX_WEIGHT * forcing / diag_sum
    for sweep in range(COARSE_SWEEPS - 1):
        guess = guess + RELAX_WEIGHT * (forcing - stencil(extend(guess), coef_pad)) / diag_sum
    residual = forcing - stencil(extend(guess), coef_pad)
    res_total, diag_total = column_total(residual, diag_sum)
    return guess + RELAX_WEIGHT * res_total / diag_total


def local_columns(residual, diag_sum):
    return (jnp.sum(residual, axis=0, keepdims=True), jnp.sum(diag_sum, axis=0, keepdims=True))


def coarsest(forcing, coef):
    column = lax.all_gather(jnp.stack([forcing, coef]), "vert", axis=1, tiled=True)

    def plane_faces(field):
        wide = extended(field, (("plane", 1),), 1)
        return jnp.pad(wide, ((1, 1), (0, 0), (1, 1)))

    whole = relax_many(column[0], column[1], plane_faces, local_columns)
    rows = forcing.shape[0]
    return lax.dynamic_slice_in_dim(whole, lax.axis_index("vert") * rows, rows, 0)


def descend(forcing, coef, depth):
    if depth == LEVELS - 1:
        return coarsest(forcing, coef)
    coef_pad = faces(coef)
    diag_sum = diagonal(coef_pad)
    guess = RELAX_WEIGHT * forcing / diag_sum
    residual = forcing - stencil(faces(guess), coef_pad)
    coarse = descend(0.5 * blocks(residual), 0.125 * blocks(coef), depth + 1)
    guess = guess + prolong(coarse)
    return guess + RELAX_WEIGHT * (forcing - stencil(faces(guess), coef_pad)) / diag_sum


def local(source, inv_density, pressure):
    stacked = extended(jnp.stack([pressure, inv_density]), (("vert", 1), ("plane", 2)), 1)
    stacked = pad_last(stacked, 1)
    guess_pad, coef_pad = (stacked[0], stacked[1])
    diag_sum = diagonal(coef_pad)
    smoothed = pressure + RELAX_WEIGHT * (source - stencil(guess_pad, coef_pad)) / diag_sum
    smoothed_pad = pad_last(extended(smoothed, (("vert", 0), ("plane", 1)), 1), 1)
    residual = source - stencil(smoothed_pad, coef_pad)
    coarse = descend(0.5 * blocks(residual), 0.125 * blocks(inv_density), 1)
    smoothed = smoothed + prolong(coarse)
    final_pad = pad_last(extended(smoothed, (("vert", 0), ("plane", 1)), 1), 1)
    return smoothed + RELAX_WEIGHT * (source - stencil(final_pad, coef_pad)) / diag_sum


def solution(mesh):
    in_specs = (P("vert", "plane", None), P("vert", "plane", None), P("vert", "plane", None))
    out_specs = P("vert", "plane", None)
    return jax.shard_map(local, mesh=mesh, in_specs=in_specs, out_specs=out_specs, check_vma=False)
```

profile of v0, /device:TPU:7, one launch (start us, length us, event | category | flops | bytes accessed | tf_op | source)
XLA Modules:
  0.0 310.7 jit_solution(1830938878676228575)
XLA Ops:
  0.8 6.4 %collective-permute-start = (f32[2,1,8,512]{3,2,1,0:T(8,128)S(1)}, f32[2,1,8,512]{3,2,1,0:T(8,128)S(1)}, u32[]{:S(2)}, u32[]{:S(2)}) collective-permute-start(f32[2,1,8,512]{3,2,1,0:T(8,128)S(1)} %get-tuple-element.21), channel_id=1, source_target_pairs={{0,1},{1,2},{2,3},{3,4},{4,5},{5,6},{6,7},{8,9},{9,10},{10,11},{11... | collective-permute-start | bytes 98312 | tf_op jit(solution)/shard_map/ppermute | solution.py:20
  7.1 1.9 collective-permute-start.1
  9.1 18.8 %reshape.99 = f32[8,2,4,2,256,2]{5,4,3,2,1,0:T(8,128)} reshape(f32[16,8,512]{2,1,0:T(8,128)} %param.4) | data formatting | bytes 524288 | tf_op jit(solution)/shard_map/reshape | solution.py:56
  27.9 7.0 %reduce_sum.87 = f32[8,4,256]{2,1,0:T(4,128)S(1)} reduce(f32[8,2,4,2,256,2]{5,4,3,2,1,0:T(8,128)} %reshape.99, f32[]{:T(128)} %constant.9.clone.1), dimensions={1,3,5}, to_apply=%region_1.2 | reduce | flops 57344 | bytes 294916 | tf_op jit(solution)/shard_map/reduce_sum | solution.py:56
  34.9 4.5 %collective-permute-start.8 = (f32[1,4,256]{2,1,0:T(4,128)S(1)}, f32[1,4,256]{2,1,0:T(4,128)S(1)}, u32[]{:S(2)}, u32[]{:S(2)}) collective-permute-start(f32[1,4,256]{2,1,0:T(4,128)S(1)} %get-tuple-element.42), channel_id=1, source_target_pairs={{0,1},{1,2},{2,3},{3,4},{4,5},{5,6},{6,7},{8,9},{9,10},{10,11},{11... | collective-permute-start | bytes 12296 | tf_op jit(solution)/shard_map/ppermute | solution.py:20
  39.5 1.9 collective-permute-start.9
  41.4 2.1 mul.490
  43.8 4.8 %collective-permute-start.16 = (f32[1,2,128]{2,0,1:T(1,128)S(1)}, f32[1,2,128]{2,0,1:T(1,128)S(1)}, u32[]{:S(2)}, u32[]{:S(2)}) collective-permute-start(f32[1,2,128]{2,0,1:T(1,128)S(1)} %get-tuple-element.57), channel_id=1, source_target_pairs={{0,1},{1,2},{2,3},{3,4},{4,5},{5,6},{6,7},{8,9},{9,10},{10,11},{11... | collective-permute-start | bytes 3080 | tf_op jit(solution)/shard_map/ppermute | solution.py:20
  48.6 1.9 collective-permute-start.17
  50.7 3.2 %collective-permute-start.2 = (f32[2,18,1,512]{3,2,1,0:T(1,128)S(1)}, f32[2,18,1,512]{3,2,1,0:T(1,128)S(1)}, u32[]{:S(2)}, u32[]{:S(2)}) collective-permute-start(f32[2,18,1,512]{3,2,1,0:T(1,128)S(1)} %get-tuple-element.19), channel_id=1, source_target_pairs={{0,8},{8,16},{16,24},{24,32},{32,40},{40,48},{48,56},{56,64},{64,7... | collective-permute-start | bytes 221192 | tf_op jit(solution)/shard_map/ppermute | solution.py:20
  53.9 5.6 %collective-permute-start.3 = (f32[2,18,1,512]{3,2,1,0:T(1,128)S(1)}, f32[2,18,1,512]{3,2,1,0:T(1,128)S(1)}, u32[]{:S(2)}, u32[]{:S(2)}) collective-permute-start(f32[2,18,1,512]{3,2,1,0:T(1,128)S(1)} %get-tuple-element.20), channel_id=1, source_target_pairs={{8,0},{16,8},{24,16},{32,24},{40,32},{48,40},{56,48},{64,56},{72,6... | collective-permute-start | bytes 221192 | tf_op jit(solution)/shard_map/ppermute | solution.py:21
  59.6 1.3 collective-permute-done.3
  60.9 0.9 select_maximum_fusion
  62.8 0.9 fusion.42
  63.8 6.3 %collective-permute-start.4 = (f32[1,8,512]{2,1,0:T(8,128)S(1)}, f32[1,8,512]{2,1,0:T(8,128)S(1)}, u32[]{:S(2)}, u32[]{:S(2)}) collective-permute-start(f32[1,8,512]{2,1,0:T(8,128)S(1)} %get-tuple-element.29), channel_id=1, source_target_pairs={{0,1},{1,2},{2,3},{3,4},{4,5},{5,6},{6,7},{8,9},{9,10},{10,11},{11... | collective-permute-start | bytes 49160 | tf_op jit(solution)/shard_map/ppermute | solution.py:20
  70.1 1.9 collective-permute-start.5
  72.1 2.1 collective-permute-start.10
  74.2 6.8 %collective-permute-start.11 = (f32[10,1,256]{2,1,0:T(1,128)S(1)}, f32[10,1,256]{2,1,0:T(1,128)S(1)}, u32[]{:S(2)}, u32[]{:S(2)}) collective-permute-start(f32[10,1,256]{2,1,0:T(1,128)S(1)} %get-tuple-element.36), channel_id=1, source_target_pairs={{8,0},{16,8},{24,16},{32,24},{40,32},{48,40},{56,48},{64,56},{72,6... | collective-permute-start | bytes 30728 | tf_op jit(solution)/shard_map/ppermute | solution.py:21
  81.1 1.9 collective-permute-start.6
  83.0 6.4 %collective-permute-start.7 = (f32[18,1,512]{2,1,0:T(1,128)S(1)}, f32[18,1,512]{2,1,0:T(1,128)S(1)}, u32[]{:S(2)}, u32[]{:S(2)}) collective-permute-start(f32[18,1,512]{2,1,0:T(1,128)S(1)} %get-tuple-element.26), channel_id=1, source_target_pairs={{8,0},{16,8},{24,16},{32,24},{40,32},{48,40},{56,48},{64,56},{72,6... | collective-permute-start | bytes 110600 | tf_op jit(solution)/shard_map/ppermute | solution.py:21
  91.5 18.1 %reshape.98 = f32[8,2,4,2,256,2]{5,4,3,2,1,0:T(8,128)} reshape(f32[16,8,512]{2,1,0:T(8,128)S(1)} %fusion.23) | data formatting | bytes 524288 | tf_op jit(solution)/shard_map/reshape | solution.py:56
  109.6 7.0 %reduce_sum.86 = f32[8,4,256]{2,1,0:T(4,128)S(1)} reduce(f32[8,2,4,2,256,2]{5,4,3,2,1,0:T(8,128)} %reshape.98, f32[]{:T(128)} %constant.9.clone.1), dimensions={1,3,5}, to_apply=%region_0.1 | reduce | flops 57344 | bytes 294916 | tf_op jit(solution)/shard_map/reduce_sum | solution.py:56
  116.7 6.0 %collective-permute-start.12 = (f32[1,4,256]{2,1,0:T(4,128)S(1)}, f32[1,4,256]{2,1,0:T(4,128)S(1)}, u32[]{:S(2)}, u32[]{:S(2)}) collective-permute-start(f32[1,4,256]{2,1,0:T(4,128)S(1)} %get-tuple-element.39), channel_id=1, source_target_pairs={{0,1},{1,2},{2,3},{3,4},{4,5},{5,6},{6,7},{8,9},{9,10},{10,11},{11... | collective-permute-start | bytes 12296 | tf_op jit(solution)/shard_map/ppermute | solution.py:20
  122.7 1.9 collective-permute-start.13
  124.6 1.9 collective-permute-start.18
  126.6 7.0 %collective-permute-start.19 = (f32[6,1,128]{2,0,1:T(8,128)S(1)}, f32[6,1,128]{2,0,1:T(8,128)S(1)}, u32[]{:S(2)}, u32[]{:S(2)}) collective-permute-start(f32[6,1,128]{2,0,1:T(8,128)S(1)} %get-tuple-element.50), channel_id=1, source_target_pairs={{8,0},{16,8},{24,16},{32,24},{40,32},{48,40},{56,48},{64,56},{72,6... | collective-permute-start | bytes 9224 | tf_op jit(solution)/shard_map/ppermute | solution.py:21
  133.6 1.9 collective-permute-start.14
  135.5 6.6 %collective-permute-start.15 = (f32[10,1,256]{2,1,0:T(1,128)S(1)}, f32[10,1,256]{2,1,0:T(1,128)S(1)}, u32[]{:S(2)}, u32[]{:S(2)}) collective-permute-start(f32[10,1,256]{2,1,0:T(1,128)S(1)} %get-tuple-element.34), channel_id=1, source_target_pairs={{8,0},{16,8},{24,16},{32,24},{40,32},{48,40},{56,48},{64,56},{72,6... | collective-permute-start | bytes 30728 | tf_op jit(solution)/shard_map/ppermute | solution.py:21
  144.5 2.8 reshape.100
  149.1 6.5 %collective-permute-start.20 = (f32[1,2,128]{2,0,1:T(1,128)S(1)}, f32[1,2,128]{2,0,1:T(1,128)S(1)}, u32[]{:S(2)}, u32[]{:S(2)}) collective-permute-start(f32[1,2,128]{2,0,1:T(1,128)S(1)} %get-tuple-element.53), channel_id=1, source_target_pairs={{0,1},{1,2},{2,3},{3,4},{4,5},{5,6},{6,7},{8,9},{9,10},{10,11},{11... | collective-permute-start | bytes 3080 | tf_op jit(solution)/shard_map/ppermute | solution.py:20
  155.6 1.9 collective-permute-start.21
  157.5 5.5 %collective-permute-done.21 = f32[1,2,128]{2,0,1:T(1,128)S(1)} collective-permute-done((f32[1,2,128]{2,0,1:T(1,128)S(1)}, f32[1,2,128]{2,0,1:T(1,128)S(1)}, u32[]{:S(2)}, u32[]{:S(2)}) %collective-permute-start.21) | collective-permute-done | bytes 1056 | tf_op jit(solution)/shard_map/ppermute | solution.py:21
  163.1 1.9 collective-permute-start.22
  165.0 6.5 %collective-permute-start.23 = (f32[6,1,128]{2,0,1:T(8,128)S(1)}, f32[6,1,128]{2,0,1:T(8,128)S(1)}, u32[]{:S(2)}, u32[]{:S(2)}) collective-permute-start(f32[6,1,128]{2,0,1:T(8,128)S(1)} %get-tuple-element.48), channel_id=1, source_target_pairs={{8,0},{16,8},{24,16},{32,24},{40,32},{48,40},{56,48},{64,56},{72,6... | collective-permute-start | bytes 9224 | tf_op jit(solution)/shard_map/ppermute | solution.py:21
  173.5 20.8 %all_gather.3 = f32[2,16,1,64]{3,0,2,1:T(2,128)S(1)} all-gather(f32[2,2,1,64]{3,0,2,1:T(2,128)S(1)} %copy.154), channel_id=1, replica_groups=mesh['plane'=64,'vert'=8] {'vert'}, dimensions={1}, use_global_device_ids=true | all-gather | bytes 9216 | tf_op jit(solution)/shard_map/all_gather | solution.py:88
  194.3 1.9 collective-permute-start.24
  196.2 6.9 %collective-permute-start.25 = (f32[16,1,64]{2,0,1:T(8,128)S(1)}, f32[16,1,64]{2,0,1:T(8,128)S(1)}, u32[]{:S(2)}, u32[]{:S(2)}) collective-permute-start(f32[16,1,64]{2,0,1:T(8,128)S(1)} %bitcast.54), channel_id=1, source_target_pairs={{8,0},{16,8},{24,16},{32,24},{40,32},{48,40},{56,48},{64,56},{72,6... | collective-permute-start | bytes 12296 | tf_op jit(solution)/shard_map/ppermute | solution.py:21
  204.1 1.9 collective-permute-start.26
  206.0 6.6 %collective-permute-start.27 = (f32[16,1,64]{2,0,1:T(8,128)S(1)}, f32[16,1,64]{2,0,1:T(8,128)S(1)}, u32[]{:S(2)}, u32[]{:S(2)}) collective-permute-start(f32[16,1,64]{2,0,1:T(8,128)S(1)} %get-tuple-element.7), channel_id=1, source_target_pairs={{8,0},{16,8},{24,16},{32,24},{40,32},{48,40},{56,48},{64,56},{72,6... | collective-permute-start | bytes 12296 | tf_op jit(solution)/shard_map/ppermute | solution.py:21
  213.6 1.9 collective-permute-start.28
  215.5 6.6 %collective-permute-start.29 = (f32[16,1,64]{2,0,1:T(8,128)S(1)}, f32[16,1,64]{2,0,1:T(8,128)S(1)}, u32[]{:S(2)}, u32[]{:S(2)}) collective-permute-start(f32[16,1,64]{2,0,1:T(8,128)S(1)} %fusion.150), channel_id=1, source_target_pairs={{8,0},{16,8},{24,16},{32,24},{40,32},{48,40},{56,48},{64,56},{72,6... | collective-permute-start | bytes 12296 | tf_op jit(solution)/shard_map/ppermute | solution.py:21
  223.1 1.9 collective-permute-start.30
  225.0 6.6 %collective-permute-start.31 = (f32[16,1,64]{2,0,1:T(8,128)S(1)}, f32[16,1,64]{2,0,1:T(8,128)S(1)}, u32[]{:S(2)}, u32[]{:S(2)}) collective-permute-start(f32[16,1,64]{2,0,1:T(8,128)S(1)} %fusion.137), channel_id=1, source_target_pairs={{8,0},{16,8},{24,16},{32,24},{40,32},{48,40},{56,48},{64,56},{72,6... | collective-permute-start | bytes 12296 | tf_op jit(solution)/shard_map/ppermute | solution.py:21
  232.7 1.9 collective-permute-start.32
  234.6 6.6 %collective-permute-start.33 = (f32[16,1,64]{2,0,1:T(8,128)S(1)}, f32[16,1,64]{2,0,1:T(8,128)S(1)}, u32[]{:S(2)}, u32[]{:S(2)}) collective-permute-start(f32[16,1,64]{2,0,1:T(8,128)S(1)} %fusion.124), channel_id=1, source_target_pairs={{8,0},{16,8},{24,16},{32,24},{40,32},{48,40},{56,48},{64,56},{72,6... | collective-permute-start | bytes 12296 | tf_op jit(solution)/shard_map/ppermute | solution.py:21
  242.4 6.0 %collective-permute-start.34 = (f32[1,2,128]{2,0,1:T(1,128)S(1)}, f32[1,2,128]{2,0,1:T(1,128)S(1)}, u32[]{:S(2)}, u32[]{:S(2)}) collective-permute-start(f32[1,2,128]{2,0,1:T(1,128)S(1)} %get-tuple-element.51), channel_id=1, source_target_pairs={{0,1},{1,2},{2,3},{3,4},{4,5},{5,6},{6,7},{8,9},{9,10},{10,11},{11... | collective-permute-start | bytes 3080 | tf_op jit(solution)/shard_map/ppermute | solution.py:20
  248.5 2.8 collective-permute-start.35
  251.3 2.9 collective-permute-done.35
  254.3 1.9 collective-permute-start.36
  256.2 6.9 %collective-permute-start.37 = (f32[6,1,128]{2,0,1:T(8,128)S(1)}, f32[6,1,128]{2,0,1:T(8,128)S(1)}, u32[]{:S(2)}, u32[]{:S(2)}) collective-permute-start(f32[6,1,128]{2,0,1:T(8,128)S(1)} %get-tuple-element.46), channel_id=1, source_target_pairs={{8,0},{16,8},{24,16},{32,24},{40,32},{48,40},{56,48},{64,56},{72,6... | collective-permute-start | bytes 9224 | tf_op jit(solution)/shard_map/ppermute | solution.py:21
  265.4 3.7 %collective-permute-start.38 = (f32[1,4,256]{2,1,0:T(4,128)S(1)}, f32[1,4,256]{2,1,0:T(4,128)S(1)}, u32[]{:S(2)}, u32[]{:S(2)}) collective-permute-start(f32[1,4,256]{2,1,0:T(4,128)S(1)} %get-tuple-element.37), channel_id=1, source_target_pairs={{0,1},{1,2},{2,3},{3,4},{4,5},{5,6},{6,7},{8,9},{9,10},{10,11},{11... | collective-permute-start | bytes 12296 | tf_op jit(solution)/shard_map/ppermute | solution.py:20
  269.2 1.9 collective-permute-start.39
  271.1 4.9 %collective-permute-done.39 = f32[1,4,256]{2,1,0:T(4,128)S(1)} collective-permute-done((f32[1,4,256]{2,1,0:T(4,128)S(1)}, f32[1,4,256]{2,1,0:T(4,128)S(1)}, u32[]{:S(2)}, u32[]{:S(2)}) %collective-permute-start.39) | collective-permute-done | bytes 4128 | tf_op jit(solution)/shard_map/ppermute | solution.py:21
  276.0 1.9 collective-permute-start.40
  277.9 6.6 %collective-permute-start.41 = (f32[10,1,256]{2,1,0:T(1,128)S(1)}, f32[10,1,256]{2,1,0:T(1,128)S(1)}, u32[]{:S(2)}, u32[]{:S(2)}) collective-permute-start(f32[10,1,256]{2,1,0:T(1,128)S(1)} %get-tuple-element.32), channel_id=1, source_target_pairs={{8,0},{16,8},{24,16},{32,24},{40,32},{48,40},{56,48},{64,56},{72,6... | collective-permute-start | bytes 30728 | tf_op jit(solution)/shard_map/ppermute | solution.py:21
  286.5 1.5 copy.161
  288.0 1.0 add.537
  289.0 3.3 %collective-permute-start.42 = (f32[1,8,512]{2,1,0:T(8,128)S(1)}, f32[1,8,512]{2,1,0:T(8,128)S(1)}, u32[]{:S(2)}, u32[]{:S(2)}) collective-permute-start(f32[1,8,512]{2,1,0:T(8,128)S(1)} %get-tuple-element.27), channel_id=1, source_target_pairs={{0,1},{1,2},{2,3},{3,4},{4,5},{5,6},{6,7},{8,9},{9,10},{10,11},{11... | collective-permute-start | bytes 49160 | tf_op jit(solution)/shard_map/ppermute | solution.py:20
  292.3 1.9 collective-permute-start.43
  294.3 5.0 %collective-permute-done.43 = f32[1,8,512]{2,1,0:T(8,128)S(1)} collective-permute-done((f32[1,8,512]{2,1,0:T(8,128)S(1)}, f32[1,8,512]{2,1,0:T(8,128)S(1)}, u32[]{:S(2)}, u32[]{:S(2)}) %collective-permute-start.43) | collective-permute-done | bytes 16416 | tf_op jit(solution)/shard_map/ppermute | solution.py:21
  299.3 1.9 collective-permute-start.44
  301.2 6.6 %collective-permute-start.45 = (f32[18,1,512]{2,1,0:T(1,128)S(1)}, f32[18,1,512]{2,1,0:T(1,128)S(1)}, u32[]{:S(2)}, u32[]{:S(2)}) collective-permute-start(f32[18,1,512]{2,1,0:T(1,128)S(1)} %get-tuple-element.24), channel_id=1, source_target_pairs={{8,0},{16,8},{24,16},{32,24},{40,32},{48,40},{56,48},{64,56},{72,6... | collective-permute-start | bytes 110600 | tf_op jit(solution)/shard_map/ppermute | solution.py:21
  307.9 1.0 collective-permute-done.45
  309.4 1.3 fusion.7
  (163 shorter events, 20.0 us)
Async XLA Ops:
  0.8 47.8 %collective-permute-start = (f32[2,1,8,512]{3,2,1,0:T(8,128)S(1)}, f32[2,1,8,512]{3,2,1,0:T(8,128)S(1)}, u32[]{:S(2)}, u32[]{:S(2)}) collective-permute-start(f32[2,1,8,512]{3,2,1,0:T(8,128)S(1)} %get-tuple-element.21), channel_id=1, source_target_pairs={{0,1},{1,2},{2,3},{3,4},{4,5},{5,6},{6,7},{8,9},{9,10},{10,11},{11... | collective-permute-start | bytes 98312 | tf_op jit(solution)/shard_map/ppermute | solution.py:20
  7.1 43.4 %collective-permute-start.1 = (f32[2,1,8,512]{3,2,1,0:T(8,128)S(1)}, f32[2,1,8,512]{3,2,1,0:T(8,128)S(1)}, u32[]{:S(2)}, u32[]{:S(2)}) collective-permute-start(f32[2,1,8,512]{3,2,1,0:T(8,128)S(1)} %get-tuple-element.22), channel_id=1, source_target_pairs={{1,0},{2,1},{3,2},{4,3},{5,4},{6,5},{7,6},{9,8},{10,9},{11,10},{12... | collective-permute-start | bytes 98312 | tf_op jit(solution)/shard_map/ppermute | solution.py:21
  34.9 108.1 %copy-start.3 = (f32[8,4,256]{2,1,0:T(4,128)}, f32[8,4,256]{2,1,0:T(4,128)S(1)}, u32[]{:S(2)}) copy-start(f32[8,4,256]{2,1,0:T(4,128)S(1)} %reduce_sum.87) | copy-start | bytes 98308
  34.9 37.1 %collective-permute-start.8 = (f32[1,4,256]{2,1,0:T(4,128)S(1)}, f32[1,4,256]{2,1,0:T(4,128)S(1)}, u32[]{:S(2)}, u32[]{:S(2)}) collective-permute-start(f32[1,4,256]{2,1,0:T(4,128)S(1)} %get-tuple-element.42), channel_id=1, source_target_pairs={{0,1},{1,2},{2,3},{3,4},{4,5},{5,6},{6,7},{8,9},{9,10},{10,11},{11... | collective-permute-start | bytes 12296 | tf_op jit(solution)/shard_map/ppermute | solution.py:20
  39.5 32.6 %collective-permute-start.9 = (f32[1,4,256]{2,1,0:T(4,128)S(1)}, f32[1,4,256]{2,1,0:T(4,128)S(1)}, u32[]{:S(2)}, u32[]{:S(2)}) collective-permute-start(f32[1,4,256]{2,1,0:T(4,128)S(1)} %get-tuple-element.41), channel_id=1, source_target_pairs={{1,0},{2,1},{3,2},{4,3},{5,4},{6,5},{7,6},{9,8},{10,9},{11,10},{12... | collective-permute-start | bytes 12296 | tf_op jit(solution)/shard_map/ppermute | solution.py:21
  43.5 7.0 %copy-start = (f32[16,8,512]{2,1,0:T(8,128)S(1)}, f32[16,8,512]{2,1,0:T(8,128)}, u32[]{:S(2)}) copy-start(f32[16,8,512]{2,1,0:T(8,128)} %param.4) | copy-start | bytes 786436
  43.8 18.1 %copy-start.13 = (f32[4,2,128]{2,0,1:T(4,128)}, f32[4,2,128]{2,0,1:T(4,128)S(1)}, u32[]{:S(2)}) copy-start(f32[4,2,128]{2,0,1:T(4,128)S(1)} %reduce_sum.89) | copy-start | bytes 12292
  43.8 10.1 %collective-permute-start.16 = (f32[1,2,128]{2,0,1:T(1,128)S(1)}, f32[1,2,128]{2,0,1:T(1,128)S(1)}, u32[]{:S(2)}, u32[]{:S(2)}) collective-permute-start(f32[1,2,128]{2,0,1:T(1,128)S(1)} %get-tuple-element.57), channel_id=1, source_target_pairs={{0,1},{1,2},{2,3},{3,4},{4,5},{5,6},{6,7},{8,9},{9,10},{10,11},{11... | collective-permute-start | bytes 3080 | tf_op jit(solution)/shard_map/ppermute | solution.py:20
  48.6 10.9 %collective-permute-start.17 = (f32[1,2,128]{2,0,1:T(1,128)S(1)}, f32[1,2,128]{2,0,1:T(1,128)S(1)}, u32[]{:S(2)}, u32[]{:S(2)}) collective-permute-start(f32[1,2,128]{2,0,1:T(1,128)S(1)} %get-tuple-element.56), channel_id=1, source_target_pairs={{1,0},{2,1},{3,2},{4,3},{5,4},{6,5},{7,6},{9,8},{10,9},{11,10},{12... | collective-permute-start | bytes 3080 | tf_op jit(solution)/shard_map/ppermute | solution.py:21
  50.7 8.9 %collective-permute-start.2 = (f32[2,18,1,512]{3,2,1,0:T(1,128)S(1)}, f32[2,18,1,512]{3,2,1,0:T(1,128)S(1)}, u32[]{:S(2)}, u32[]{:S(2)}) collective-permute-start(f32[2,18,1,512]{3,2,1,0:T(1,128)S(1)} %get-tuple-element.19), channel_id=1, source_target_pairs={{0,8},{8,16},{16,24},{24,32},{32,40},{40,48},{48,56},{56,64},{64,7... | collective-permute-start | bytes 221192 | tf_op jit(solution)/shard_map/ppermute | solution.py:20
  53.9 88.2 %copy-start.16 = (f32[1,2,128]{2,0,1:T(1,128)}, f32[1,2,128]{2,0,1:T(1,128)S(1)}, u32[]{:S(2)}) copy-start(f32[1,2,128]{2,0,1:T(1,128)S(1)} %collective-permute-done.16) | copy-start | bytes 3076
  53.9 7.0 %collective-permute-start.3 = (f32[2,18,1,512]{3,2,1,0:T(1,128)S(1)}, f32[2,18,1,512]{3,2,1,0:T(1,128)S(1)}, u32[]{:S(2)}, u32[]{:S(2)}) collective-permute-start(f32[2,18,1,512]{3,2,1,0:T(1,128)S(1)} %get-tuple-element.20), channel_id=1, source_target_pairs={{8,0},{16,8},{24,16},{32,24},{40,32},{48,40},{56,48},{64,56},{72,6... | collective-permute-start | bytes 221192 | tf_op jit(solution)/shard_map/ppermute | solution.py:21
  59.6 82.6 %copy-start.18 = (f32[1,2,128]{2,0,1:T(1,128)}, f32[1,2,128]{2,0,1:T(1,128)S(1)}, u32[]{:S(2)}) copy-start(f32[1,2,128]{2,0,1:T(1,128)S(1)} %collective-permute-done.17) | copy-start | bytes 3076
  63.8 17.3 %collective-permute-start.4 = (f32[1,8,512]{2,1,0:T(8,128)S(1)}, f32[1,8,512]{2,1,0:T(8,128)S(1)}, u32[]{:S(2)}, u32[]{:S(2)}) collective-permute-start(f32[1,8,512]{2,1,0:T(8,128)S(1)} %get-tuple-element.29), channel_id=1, source_target_pairs={{0,1},{1,2},{2,3},{3,4},{4,5},{5,6},{6,7},{8,9},{9,10},{10,11},{11... | collective-permute-start | bytes 49160 | tf_op jit(solution)/shard_map/ppermute | solution.py:20
  70.1 10.9 %collective-permute-start.5 = (f32[1,8,512]{2,1,0:T(8,128)S(1)}, f32[1,8,512]{2,1,0:T(8,128)S(1)}, u32[]{:S(2)}, u32[]{:S(2)}) collective-permute-start(f32[1,8,512]{2,1,0:T(8,128)S(1)} %get-tuple-element.30), channel_id=1, source_target_pairs={{1,0},{2,1},{3,2},{4,3},{5,4},{6,5},{7,6},{9,8},{10,9},{11,10},{12... | collective-permute-start | bytes 49160 | tf_op jit(solution)/shard_map/ppermute | solution.py:21
  72.0 44.5 %copy-start.11 = (f32[1,4,256]{2,1,0:T(4,128)}, f32[1,4,256]{2,1,0:T(4,128)S(1)}, u32[]{:S(2)}) copy-start(f32[1,4,256]{2,1,0:T(4,128)S(1)} %collective-permute-done.9) | copy-start | bytes 12292
  72.1 17.3 %collective-permute-start.10 = (f32[10,1,256]{2,1,0:T(1,128)S(1)}, f32[10,1,256]{2,1,0:T(1,128)S(1)}, u32[]{:S(2)}, u32[]{:S(2)}) collective-permute-start(f32[10,1,256]{2,1,0:T(1,128)S(1)} %get-tuple-element.35), channel_id=1, source_target_pairs={{0,8},{8,16},{16,24},{24,32},{32,40},{40,48},{48,56},{56,64},{64,7... | collective-permute-start | bytes 30728 | tf_op jit(solution)/shard_map/ppermute | solution.py:20
  74.2 15.2 %collective-permute-start.11 = (f32[10,1,256]{2,1,0:T(1,128)S(1)}, f32[10,1,256]{2,1,0:T(1,128)S(1)}, u32[]{:S(2)}, u32[]{:S(2)}) collective-permute-start(f32[10,1,256]{2,1,0:T(1,128)S(1)} %get-tuple-element.36), channel_id=1, source_target_pairs={{8,0},{16,8},{24,16},{32,24},{40,32},{48,40},{56,48},{64,56},{72,6... | collective-permute-start | bytes 30728 | tf_op jit(solution)/shard_map/ppermute | solution.py:21
  81.1 8.5 %collective-permute-start.6 = (f32[18,1,512]{2,1,0:T(1,128)S(1)}, f32[18,1,512]{2,1,0:T(1,128)S(1)}, u32[]{:S(2)}, u32[]{:S(2)}) collective-permute-start(f32[18,1,512]{2,1,0:T(1,128)S(1)} %get-tuple-element.25), channel_id=1, source_target_pairs={{0,8},{8,16},{16,24},{24,32},{32,40},{40,48},{48,56},{56,64},{64,7... | collective-permute-start | bytes 110600 | tf_op jit(solution)/shard_map/ppermute | solution.py:20
  83.0 7.4 %collective-permute-start.7 = (f32[18,1,512]{2,1,0:T(1,128)S(1)}, f32[18,1,512]{2,1,0:T(1,128)S(1)}, u32[]{:S(2)}, u32[]{:S(2)}) collective-permute-start(f32[18,1,512]{2,1,0:T(1,128)S(1)} %get-tuple-element.26), channel_id=1, source_target_pairs={{8,0},{16,8},{24,16},{32,24},{40,32},{48,40},{56,48},{64,56},{72,6... | collective-permute-start | bytes 110600 | tf_op jit(solution)/shard_map/ppermute | solution.py:21
  89.4 53.6 %copy-start.7 = (f32[10,1,256]{2,1,0:T(1,128)}, f32[10,1,256]{2,1,0:T(1,128)S(1)}, u32[]{:S(2)}) copy-start(f32[10,1,256]{2,1,0:T(1,128)S(1)} %collective-permute-done.10) | copy-start | bytes 30724
  89.4 53.6 %copy-start.9 = (f32[10,1,256]{2,1,0:T(1,128)}, f32[10,1,256]{2,1,0:T(1,128)S(1)}, u32[]{:S(2)}) copy-start(f32[10,1,256]{2,1,0:T(1,128)S(1)} %collective-permute-done.11) | copy-start | bytes 30724
  116.6 27.3 %copy-start.5 = (f32[8,4,256]{2,1,0:T(4,128)}, f32[8,4,256]{2,1,0:T(4,128)S(1)}, u32[]{:S(2)}) copy-start(f32[8,4,256]{2,1,0:T(4,128)S(1)} %reduce_sum.86) | copy-start | bytes 98308
  116.7 16.8 %collective-permute-start.12 = (f32[1,4,256]{2,1,0:T(4,128)S(1)}, f32[1,4,256]{2,1,0:T(4,128)S(1)}, u32[]{:S(2)}, u32[]{:S(2)}) collective-permute-start(f32[1,4,256]{2,1,0:T(4,128)S(1)} %get-tuple-element.39), channel_id=1, source_target_pairs={{0,1},{1,2},{2,3},{3,4},{4,5},{5,6},{6,7},{8,9},{9,10},{10,11},{11... | collective-permute-start | bytes 12296 | tf_op jit(solution)/shard_map/ppermute | solution.py:20
  122.7 10.8 %collective-permute-start.13 = (f32[1,4,256]{2,1,0:T(4,128)S(1)}, f32[1,4,256]{2,1,0:T(4,128)S(1)}, u32[]{:S(2)}, u32[]{:S(2)}) collective-permute-start(f32[1,4,256]{2,1,0:T(4,128)S(1)} %get-tuple-element.40), channel_id=1, source_target_pairs={{1,0},{2,1},{3,2},{4,3},{5,4},{6,5},{7,6},{9,8},{10,9},{11,10},{12... | collective-permute-start | bytes 12296 | tf_op jit(solution)/shard_map/ppermute | solution.py:21
  124.6 17.4 %collective-permute-start.18 = (f32[6,1,128]{2,0,1:T(8,128)S(1)}, f32[6,1,128]{2,0,1:T(8,128)S(1)}, u32[]{:S(2)}, u32[]{:S(2)}) collective-permute-start(f32[6,1,128]{2,0,1:T(8,128)S(1)} %get-tuple-element.49), channel_id=1, source_target_pairs={{0,8},{8,16},{16,24},{24,32},{32,40},{40,48},{48,56},{56,64},{64,7... | collective-permute-start | bytes 9224 | tf_op jit(solution)/shard_map/ppermute | solution.py:20
  126.6 15.5 %collective-permute-start.19 = (f32[6,1,128]{2,0,1:T(8,128)S(1)}, f32[6,1,128]{2,0,1:T(8,128)S(1)}, u32[]{:S(2)}, u32[]{:S(2)}) collective-permute-start(f32[6,1,128]{2,0,1:T(8,128)S(1)} %get-tuple-element.50), channel_id=1, source_target_pairs={{8,0},{16,8},{24,16},{32,24},{40,32},{48,40},{56,48},{64,56},{72,6... | collective-permute-start | bytes 9224 | tf_op jit(solution)/shard_map/ppermute | solution.py:21
  133.6 9.3 %collective-permute-start.14 = (f32[10,1,256]{2,1,0:T(1,128)S(1)}, f32[10,1,256]{2,1,0:T(1,128)S(1)}, u32[]{:S(2)}, u32[]{:S(2)}) collective-permute-start(f32[10,1,256]{2,1,0:T(1,128)S(1)} %get-tuple-element.33), channel_id=1, source_target_pairs={{0,8},{8,16},{16,24},{24,32},{32,40},{40,48},{48,56},{56,64},{64,7... | collective-permute-start | bytes 30728 | tf_op jit(solution)/shard_map/ppermute | solution.py:20
  135.5 7.3 %collective-permute-start.15 = (f32[10,1,256]{2,1,0:T(1,128)S(1)}, f32[10,1,256]{2,1,0:T(1,128)S(1)}, u32[]{:S(2)}, u32[]{:S(2)}) collective-permute-start(f32[10,1,256]{2,1,0:T(1,128)S(1)} %get-tuple-element.34), channel_id=1, source_target_pairs={{8,0},{16,8},{24,16},{32,24},{40,32},{48,40},{56,48},{64,56},{72,6... | collective-permute-start | bytes 30728 | tf_op jit(solution)/shard_map/ppermute | solution.py:21
  148.2 115.8 %copy-start.14 = (f32[4,2,128]{2,0,1:T(4,128)S(1)}, f32[4,2,128]{2,0,1:T(4,128)}, u32[]{:S(2)}) copy-start(f32[4,2,128]{2,0,1:T(4,128)} %copy-done.13) | copy-start | bytes 12292
  148.2 115.8 %copy-start.15 = (f32[4,2,128]{2,0,1:T(4,128)S(1)}, f32[4,2,128]{2,0,1:T(4,128)}, u32[]{:S(2)}) copy-start(f32[4,2,128]{2,0,1:T(4,128)} %reduce_sum.88) | copy-start | bytes 12292
  148.2 115.8 %copy-start.17 = (f32[1,2,128]{2,0,1:T(1,128)S(1)}, f32[1,2,128]{2,0,1:T(1,128)}, u32[]{:S(2)}) copy-start(f32[1,2,128]{2,0,1:T(1,128)} %copy-done.16) | copy-start | bytes 3076
  148.2 115.8 %copy-start.19 = (f32[1,2,128]{2,0,1:T(1,128)S(1)}, f32[1,2,128]{2,0,1:T(1,128)}, u32[]{:S(2)}) copy-start(f32[1,2,128]{2,0,1:T(1,128)} %copy-done.18) | copy-start | bytes 3076
  149.1 8.4 %collective-permute-start.20 = (f32[1,2,128]{2,0,1:T(1,128)S(1)}, f32[1,2,128]{2,0,1:T(1,128)S(1)}, u32[]{:S(2)}, u32[]{:S(2)}) collective-permute-start(f32[1,2,128]{2,0,1:T(1,128)S(1)} %get-tuple-element.53), channel_id=1, source_target_pairs={{0,1},{1,2},{2,3},{3,4},{4,5},{5,6},{6,7},{8,9},{9,10},{10,11},{11... | collective-permute-start | bytes 3080 | tf_op jit(solution)/shard_map/ppermute | solution.py:20
  155.6 7.5 %collective-permute-start.21 = (f32[1,2,128]{2,0,1:T(1,128)S(1)}, f32[1,2,128]{2,0,1:T(1,128)S(1)}, u32[]{:S(2)}, u32[]{:S(2)}) collective-permute-start(f32[1,2,128]{2,0,1:T(1,128)S(1)} %get-tuple-element.54), channel_id=1, source_target_pairs={{1,0},{2,1},{3,2},{4,3},{5,4},{6,5},{7,6},{9,8},{10,9},{11,10},{12... | collective-permute-start | bytes 3080 | tf_op jit(solution)/shard_map/ppermute | solution.py:21
  163.1 8.6 %collective-permute-start.22 = (f32[6,1,128]{2,0,1:T(8,128)S(1)}, f32[6,1,128]{2,0,1:T(8,128)S(1)}, u32[]{:S(2)}, u32[]{:S(2)}) collective-permute-start(f32[6,1,128]{2,0,1:T(8,128)S(1)} %get-tuple-element.47), channel_id=1, source_target_pairs={{0,8},{8,16},{16,24},{24,32},{32,40},{40,48},{48,56},{56,64},{64,7... | collective-permute-start | bytes 9224 | tf_op jit(solution)/shard_map/ppermute | solution.py:20
  165.0 7.2 %collective-permute-start.23 = (f32[6,1,128]{2,0,1:T(8,128)S(1)}, f32[6,1,128]{2,0,1:T(8,128)S(1)}, u32[]{:S(2)}, u32[]{:S(2)}) collective-permute-start(f32[6,1,128]{2,0,1:T(8,128)S(1)} %get-tuple-element.48), channel_id=1, source_target_pairs={{8,0},{16,8},{24,16},{32,24},{40,32},{48,40},{56,48},{64,56},{72,6... | collective-permute-start | bytes 9224 | tf_op jit(solution)/shard_map/ppermute | solution.py:21
  194.3 8.9 %collective-permute-start.24 = (f32[16,1,64]{2,0,1:T(8,128)S(1)}, f32[16,1,64]{2,0,1:T(8,128)S(1)}, u32[]{:S(2)}, u32[]{:S(2)}) collective-permute-start(f32[16,1,64]{2,0,1:T(8,128)S(1)} %bitcast.53), channel_id=1, source_target_pairs={{0,8},{8,16},{16,24},{24,32},{32,40},{40,48},{48,56},{56,64},{64,7... | collective-permute-start | bytes 12296 | tf_op jit(solution)/shard_map/ppermute | solution.py:20
  196.2 7.7 %collective-permute-start.25 = (f32[16,1,64]{2,0,1:T(8,128)S(1)}, f32[16,1,64]{2,0,1:T(8,128)S(1)}, u32[]{:S(2)}, u32[]{:S(2)}) collective-permute-start(f32[16,1,64]{2,0,1:T(8,128)S(1)} %bitcast.54), channel_id=1, source_target_pairs={{8,0},{16,8},{24,16},{32,24},{40,32},{48,40},{56,48},{64,56},{72,6... | collective-permute-start | bytes 12296 | tf_op jit(solution)/shard_map/ppermute | solution.py:21
  204.1 8.6 %collective-permute-start.26 = (f32[16,1,64]{2,0,1:T(8,128)S(1)}, f32[16,1,64]{2,0,1:T(8,128)S(1)}, u32[]{:S(2)}, u32[]{:S(2)}) collective-permute-start(f32[16,1,64]{2,0,1:T(8,128)S(1)} %get-tuple-element.7), channel_id=1, source_target_pairs={{0,8},{8,16},{16,24},{24,32},{32,40},{40,48},{48,56},{56,64},{64,7... | collective-permute-start | bytes 12296 | tf_op jit(solution)/shard_map/ppermute | solution.py:20
  206.0 7.4 %collective-permute-start.27 = (f32[16,1,64]{2,0,1:T(8,128)S(1)}, f32[16,1,64]{2,0,1:T(8,128)S(1)}, u32[]{:S(2)}, u32[]{:S(2)}) collective-permute-start(f32[16,1,64]{2,0,1:T(8,128)S(1)} %get-tuple-element.7), channel_id=1, source_target_pairs={{8,0},{16,8},{24,16},{32,24},{40,32},{48,40},{56,48},{64,56},{72,6... | collective-permute-start | bytes 12296 | tf_op jit(solution)/shard_map/ppermute | solution.py:21
  213.6 8.6 %collective-permute-start.28 = (f32[16,1,64]{2,0,1:T(8,128)S(1)}, f32[16,1,64]{2,0,1:T(8,128)S(1)}, u32[]{:S(2)}, u32[]{:S(2)}) collective-permute-start(f32[16,1,64]{2,0,1:T(8,128)S(1)} %fusion.150), channel_id=1, source_target_pairs={{0,8},{8,16},{16,24},{24,32},{32,40},{40,48},{48,56},{56,64},{64,7... | collective-permute-start | bytes 12296 | tf_op jit(solution)/shard_map/ppermute | solution.py:20
  215.5 7.4 %collective-permute-start.29 = (f32[16,1,64]{2,0,1:T(8,128)S(1)}, f32[16,1,64]{2,0,1:T(8,128)S(1)}, u32[]{:S(2)}, u32[]{:S(2)}) collective-permute-start(f32[16,1,64]{2,0,1:T(8,128)S(1)} %fusion.150), channel_id=1, source_target_pairs={{8,0},{16,8},{24,16},{32,24},{40,32},{48,40},{56,48},{64,56},{72,6... | collective-permute-start | bytes 12296 | tf_op jit(solution)/shard_map/ppermute | solution.py:21
  223.1 8.6 %collective-permute-start.30 = (f32[16,1,64]{2,0,1:T(8,128)S(1)}, f32[16,1,64]{2,0,1:T(8,128)S(1)}, u32[]{:S(2)}, u32[]{:S(2)}) collective-permute-start(f32[16,1,64]{2,0,1:T(8,128)S(1)} %fusion.137), channel_id=1, source_target_pairs={{0,8},{8,16},{16,24},{24,32},{32,40},{40,48},{48,56},{56,64},{64,7... | collective-permute-start | bytes 12296 | tf_op jit(solution)/shard_map/ppermute | solution.py:20
  225.0 7.4 %collective-permute-start.31 = (f32[16,1,64]{2,0,1:T(8,128)S(1)}, f32[16,1,64]{2,0,1:T(8,128)S(1)}, u32[]{:S(2)}, u32[]{:S(2)}) collective-permute-start(f32[16,1,64]{2,0,1:T(8,128)S(1)} %fusion.137), channel_id=1, source_target_pairs={{8,0},{16,8},{24,16},{32,24},{40,32},{48,40},{56,48},{64,56},{72,6... | collective-permute-start | bytes 12296 | tf_op jit(solution)/shard_map/ppermute | solution.py:21
  232.5 53.0 %copy-start.4 = (f32[8,4,256]{2,1,0:T(4,128)S(1)}, f32[8,4,256]{2,1,0:T(4,128)}, u32[]{:S(2)}) copy-start(f32[8,4,256]{2,1,0:T(4,128)} %copy-done.3) | copy-start | bytes 98308
  232.5 53.0 %copy-start.6 = (f32[8,4,256]{2,1,0:T(4,128)S(1)}, f32[8,4,256]{2,1,0:T(4,128)}, u32[]{:S(2)}) copy-start(f32[8,4,256]{2,1,0:T(4,128)} %copy-done.5) | copy-start | bytes 98308
  232.6 53.0 %copy-start.8 = (f32[10,1,256]{2,1,0:T(1,128)S(1)}, f32[10,1,256]{2,1,0:T(1,128)}, u32[]{:S(2)}) copy-start(f32[10,1,256]{2,1,0:T(1,128)} %copy-done.7) | copy-start | bytes 30724
  232.6 53.0 %copy-start.10 = (f32[10,1,256]{2,1,0:T(1,128)S(1)}, f32[10,1,256]{2,1,0:T(1,128)}, u32[]{:S(2)}) copy-start(f32[10,1,256]{2,1,0:T(1,128)} %copy-done.9) | copy-start | bytes 30724
  232.6 53.0 %copy-start.12 = (f32[1,4,256]{2,1,0:T(4,128)S(1)}, f32[1,4,256]{2,1,0:T(4,128)}, u32[]{:S(2)}) copy-start(f32[1,4,256]{2,1,0:T(4,128)} %copy-done.11) | copy-start | bytes 12292
  232.7 8.6 %collective-permute-start.32 = (f32[16,1,64]{2,0,1:T(8,128)S(1)}, f32[16,1,64]{2,0,1:T(8,128)S(1)}, u32[]{:S(2)}, u32[]{:S(2)}) collective-permute-start(f32[16,1,64]{2,0,1:T(8,128)S(1)} %fusion.124), channel_id=1, source_target_pairs={{0,8},{8,16},{16,24},{24,32},{32,40},{40,48},{48,56},{56,64},{64,7... | collective-permute-start | bytes 12296 | tf_op jit(solution)/shard_map/ppermute | solution.py:20
  234.6 7.4 %collective-permute-start.33 = (f32[16,1,64]{2,0,1:T(8,128)S(1)}, f32[16,1,64]{2,0,1:T(8,128)S(1)}, u32[]{:S(2)}, u32[]{:S(2)}) collective-permute-start(f32[16,1,64]{2,0,1:T(8,128)S(1)} %fusion.124), channel_id=1, source_target_pairs={{8,0},{16,8},{24,16},{32,24},{40,32},{48,40},{56,48},{64,56},{72,6... | collective-permute-start | bytes 12296 | tf_op jit(solution)/shard_map/ppermute | solution.py:21
  242.4 8.9 %collective-permute-start.34 = (f32[1,2,128]{2,0,1:T(1,128)S(1)}, f32[1,2,128]{2,0,1:T(1,128)S(1)}, u32[]{:S(2)}, u32[]{:S(2)}) collective-permute-start(f32[1,2,128]{2,0,1:T(1,128)S(1)} %get-tuple-element.51), channel_id=1, source_target_pairs={{0,1},{1,2},{2,3},{3,4},{4,5},{5,6},{6,7},{8,9},{9,10},{10,11},{11... | collective-permute-start | bytes 3080 | tf_op jit(solution)/shard_map/ppermute | solution.py:20
  248.5 5.8 %collective-permute-start.35 = (f32[1,2,128]{2,0,1:T(1,128)S(1)}, f32[1,2,128]{2,0,1:T(1,128)S(1)}, u32[]{:S(2)}, u32[]{:S(2)}) collective-permute-start(f32[1,2,128]{2,0,1:T(1,128)S(1)} %get-tuple-element.52), channel_id=1, source_target_pairs={{1,0},{2,1},{3,2},{4,3},{5,4},{6,5},{7,6},{9,8},{10,9},{11,10},{12... | collective-permute-start | bytes 3080 | tf_op jit(solution)/shard_map/ppermute | solution.py:21
  254.3 8.9 %collective-permute-start.36 = (f32[6,1,128]{2,0,1:T(8,128)S(1)}, f32[6,1,128]{2,0,1:T(8,128)S(1)}, u32[]{:S(2)}, u32[]{:S(2)}) collective-permute-start(f32[6,1,128]{2,0,1:T(8,128)S(1)} %get-tuple-element.45), channel_id=1, source_target_pairs={{0,8},{8,16},{16,24},{24,32},{32,40},{40,48},{48,56},{56,64},{64,7... | collective-permute-start | bytes 9224 | tf_op jit(solution)/shard_map/ppermute | solution.py:20
  256.2 7.7 %collective-permute-start.37 = (f32[6,1,128]{2,0,1:T(8,128)S(1)}, f32[6,1,128]{2,0,1:T(8,128)S(1)}, u32[]{:S(2)}, u32[]{:S(2)}) collective-permute-start(f32[6,1,128]{2,0,1:T(8,128)S(1)} %get-tuple-element.46), channel_id=1, source_target_pairs={{8,0},{16,8},{24,16},{32,24},{40,32},{48,40},{56,48},{64,56},{72,6... | collective-permute-start | bytes 9224 | tf_op jit(solution)/shard_map/ppermute | solution.py:21
  265.4 5.6 %collective-permute-start.38 = (f32[1,4,256]{2,1,0:T(4,128)S(1)}, f32[1,4,256]{2,1,0:T(4,128)S(1)}, u32[]{:S(2)}, u32[]{:S(2)}) collective-permute-start(f32[1,4,256]{2,1,0:T(4,128)S(1)} %get-tuple-element.37), channel_id=1, source_target_pairs={{0,1},{1,2},{2,3},{3,4},{4,5},{5,6},{6,7},{8,9},{9,10},{10,11},{11... | collective-permute-start | bytes 12296 | tf_op jit(solution)/shard_map/ppermute | solution.py:20
  269.2 6.8 %collective-permute-start.39 = (f32[1,4,256]{2,1,0:T(4,128)S(1)}, f32[1,4,256]{2,1,0:T(4,128)S(1)}, u32[]{:S(2)}, u32[]{:S(2)}) collective-permute-start(f32[1,4,256]{2,1,0:T(4,128)S(1)} %get-tuple-element.38), channel_id=1, source_target_pairs={{1,0},{2,1},{3,2},{4,3},{5,4},{6,5},{7,6},{9,8},{10,9},{11,10},{12... | collective-permute-start | bytes 12296 | tf_op jit(solution)/shard_map/ppermute | solution.py:21
  276.0 8.6 %collective-permute-start.40 = (f32[10,1,256]{2,1,0:T(1,128)S(1)}, f32[10,1,256]{2,1,0:T(1,128)S(1)}, u32[]{:S(2)}, u32[]{:S(2)}) collective-permute-start(f32[10,1,256]{2,1,0:T(1,128)S(1)} %get-tuple-element.31), channel_id=1, source_target_pairs={{0,8},{8,16},{16,24},{24,32},{32,40},{40,48},{48,56},{56,64},{64,7... | collective-permute-start | bytes 30728 | tf_op jit(solution)/shard_map/ppermute | solution.py:20
  277.9 7.4 %collective-permute-start.41 = (f32[10,1,256]{2,1,0:T(1,128)S(1)}, f32[10,1,256]{2,1,0:T(1,128)S(1)}, u32[]{:S(2)}, u32[]{:S(2)}) collective-permute-start(f32[10,1,256]{2,1,0:T(1,128)S(1)} %get-tuple-element.32), channel_id=1, source_target_pairs={{8,0},{16,8},{24,16},{32,24},{40,32},{48,40},{56,48},{64,56},{72,6... | collective-permute-start | bytes 30728 | tf_op jit(solution)/shard_map/ppermute | solution.py:21
  289.0 5.3 %collective-permute-start.42 = (f32[1,8,512]{2,1,0:T(8,128)S(1)}, f32[1,8,512]{2,1,0:T(8,128)S(1)}, u32[]{:S(2)}, u32[]{:S(2)}) collective-permute-start(f32[1,8,512]{2,1,0:T(8,128)S(1)} %get-tuple-element.27), channel_id=1, source_target_pairs={{0,1},{1,2},{2,3},{3,4},{4,5},{5,6},{6,7},{8,9},{9,10},{10,11},{11... | collective-permute-start | bytes 49160 | tf_op jit(solution)/shard_map/ppermute | solution.py:20
  292.3 6.9 %collective-permute-start.43 = (f32[1,8,512]{2,1,0:T(8,128)S(1)}, f32[1,8,512]{2,1,0:T(8,128)S(1)}, u32[]{:S(2)}, u32[]{:S(2)}) collective-permute-start(f32[1,8,512]{2,1,0:T(8,128)S(1)} %get-tuple-element.28), channel_id=1, source_target_pairs={{1,0},{2,1},{3,2},{4,3},{5,4},{6,5},{7,6},{9,8},{10,9},{11,10},{12... | collective-permute-start | bytes 49160 | tf_op jit(solution)/shard_map/ppermute | solution.py:21
  299.3 8.6 %collective-permute-start.44 = (f32[18,1,512]{2,1,0:T(1,128)S(1)}, f32[18,1,512]{2,1,0:T(1,128)S(1)}, u32[]{:S(2)}, u32[]{:S(2)}) collective-permute-start(f32[18,1,512]{2,1,0:T(1,128)S(1)} %get-tuple-element.23), channel_id=1, source_target_pairs={{0,8},{8,16},{16,24},{24,32},{32,40},{40,48},{48,56},{56,64},{64,7... | collective-permute-start | bytes 110600 | tf_op jit(solution)/shard_map/ppermute | solution.py:20
  301.2 7.7 %collective-permute-start.45 = (f32[18,1,512]{2,1,0:T(1,128)S(1)}, f32[18,1,512]{2,1,0:T(1,128)S(1)}, u32[]{:S(2)}, u32[]{:S(2)}) collective-permute-start(f32[18,1,512]{2,1,0:T(1,128)S(1)} %get-tuple-element.24), channel_id=1, source_target_pairs={{8,0},{16,8},{24,16},{32,24},{40,32},{48,40},{56,48},{64,56},{72,6... | collective-permute-start | bytes 110600 | tf_op jit(solution)/shard_map/ppermute | solution.py:21
  (4 other events, 9.5 us)
where the time goes:
time: 313 us; the launch traced here: 311 us
  starting transfers between devices  186 us (59%)
  local copies, waits for them, and re-layouts  46.8 us (15%)
  other arithmetic  28 us (9%)
  waiting for transfers between devices  27.4 us (9%)
  blocking collectives  20.8 us (7%)
    ppermute x23, starting transfers between devices, extended(): after = lax.ppermute(first, axis, down)  111 us
    ppermute x23, starting transfers between devices, extended(): before = lax.ppermute(last, axis, up)  75.8 us
    reshape x3, local copies, waits for them, and re-layouts, blocks(): return field.reshape(a // 2, 2, b // 2, 2, c // 2, 2).sum(axis=(1, 3, 5))  39.8 us
    ppermute x23, waiting for transfers between devices, extended(): after = lax.ppermute(first, axis, down)  27.3 us
    all_gather x1, blocking collectives, coarsest(): lax.all_gather(jnp.stack([forcing, coef]), 'vert', axis=1, tiled=True)  20.8 us
    reduce_sum x7, other arithmetic, blocks(): return field.reshape(a // 2, 2, b // 2, 2, c // 2, 2).sum(axis=(1, 3, 5))  16.1 us
  transfers between devices with their start and end apart: 46, of which 15 were waited for; matrix products, arithmetic and copies ran while one was open for 10% of the time, Pallas kernels for 0%

commit v1 on v0

v1 whole, which is shorter than its diff:
```python
import functools

import jax
import jax.numpy as jnp
from jax import lax
from jax.experimental import pallas as pl
from jax.experimental.pallas import tpu as pltpu
from jax.sharding import PartitionSpec as P

COARSE_SWEEPS = 4
RELAX_WEIGHT = 0.8
KEEP = 1.0 - RELAX_WEIGHT
MESH = pl.DeviceIdType.MESH
CHUNK = 4
SUB = 8

EXCHANGES = ("vin", "b0", "b1", "b2", "v0", "v1", "v2", "u2", "u1", "u0")
LEVEL_OF = {"vin": 0, "b0": 0, "b1": 1, "b2": 2, "v0": 0, "v1": 1, "v2": 2, "u2": 2, "u1": 1, "u0": 0}
SIDES = ("bc", "s0", "s1", "s2", "s3")
GATHERS = ("gb", "gf")


def scratch_plan(depth, lanes, peers):
    plan = {}
    field = lambda planes: pltpu.VMEM((planes * SUB, lanes), jnp.float32)
    for k in range(3):
        z = depth >> k
        for name in ("g", "t", "w", "d", "cym", "cyp", "cxm", "cxp", "ch"):
            plan[name + str(k)] = field(z)
        plan["cz" + str(k)] = field(z + 1)
        for name in ("b", "v", "u"):
            plan[name + str(k)] = field(z + 2)
    plan["vin"] = field(depth + 2)
    for name in EXCHANGES:
        z = depth >> LEVEL_OF[name]
        plan["hx_" + name] = pltpu.VMEM((2, z, lanes), jnp.float32)
        plan["sx_" + name] = pltpu.VMEM((2, z, lanes), jnp.float32)
        plan["hz_" + name] = pltpu.VMEM((2, SUB, lanes), jnp.float32)
    column = 2 * peers
    for name in SIDES:
        plan["hx_" + name] = pltpu.VMEM((2, column, lanes), jnp.float32)
        plan["sx_" + name] = pltpu.VMEM((column, lanes), jnp.float32)
    for name in GATHERS:
        plan["all_" + name] = pltpu.VMEM((peers * SUB, lanes), jnp.float32)
        plan["own_" + name] = pltpu.VMEM((SUB, lanes), jnp.float32)
    plan["r2"] = field(depth >> 2)
    plan["r1"] = field(depth >> 1)
    plan["col"] = pltpu.VMEM((column, lanes), jnp.float32)
    count = 4 * len(EXCHANGES) + 2 * len(SIDES) + (peers - 1) * len(GATHERS)
    plan["send"] = pltpu.SemaphoreType.DMA((count,))
    plan["recv"] = pltpu.SemaphoreType.DMA((count,))
    plan["load"] = pltpu.SemaphoreType.DMA((3,))
    return plan


def cycle_kernel(names, depth, lanes, planes, peers, source, density, pressure, out, *scratch):
    m = dict(zip(names, scratch))
    p, q = lax.axis_index("plane"), lax.axis_index("vert")
    left, right = lax.rem(p + planes - 1, planes), lax.rem(p + 1, planes)
    below, above = lax.rem(q + peers - 1, peers), lax.rem(q + 1, peers)
    p_lo = jnp.where(p == 0, 0.0, 1.0).astype(jnp.float32)
    p_hi = jnp.where(p == planes - 1, 0.0, 1.0).astype(jnp.float32)
    q_lo = jnp.where(q == 0, 0.0, 1.0).astype(jnp.float32)
    q_hi = jnp.where(q == peers - 1, 0.0, 1.0).astype(jnp.float32)

    loads = []
    for i, (src, dst) in enumerate(((density, m["b0"].at[pl.ds(SUB, SUB * depth)]),
                                    (pressure, m["vin"].at[pl.ds(SUB, SUB * depth)]),
                                    (source, m["g0"]))):
        loads.append(pltpu.make_async_copy(src, dst, m["load"].at[i]))
        loads[-1].start()

    barrier = pltpu.get_barrier_semaphore()
    for peer in (left, right):
        pl.semaphore_signal(barrier, inc=1, device_id={"plane": peer}, device_id_type=MESH)
    for step in range(1, peers):
        pl.semaphore_signal(barrier, inc=1, device_id={"vert": lax.rem(q + step, peers)}, device_id_type=MESH)

    zero = jnp.zeros((SUB, lanes), jnp.float32)
    for name in ("vin", "v0", "v1", "v2", "u0", "u1", "u2"):
        z = depth >> LEVEL_OF[name]
        m[name][pl.ds(0, SUB), :] = zero
        m[name][pl.ds(SUB * (z + 1), SUB), :] = zero

    lane = lax.broadcasted_iota(jnp.int32, (SUB, lanes), 1)
    sub = lax.broadcasted_iota(jnp.int32, (SUB, lanes), 0)

    used = [0]
    pending = {}
    started = []

    def remote(key, src, dst, device):
        at = used[0]
        used[0] += 1
        copy = pltpu.make_async_remote_copy(
            src_ref=src, dst_ref=dst, send_sem=m["send"].at[at], recv_sem=m["recv"].at[at],
            device_id=device, device_id_type=MESH)
        copy.start()
        pending.setdefault(key, []).append(copy)
        started.append(copy)

    def arrive(key):
        for copy in pending.pop(key):
            copy.wait_recv()

    def exchange(name, field):
        z = depth >> LEVEL_OF[name]
        hx, sx, hz = m["hx_" + name], m["sx_" + name], m["hz_" + name]
        remote(name, field.at[pl.ds(SUB, SUB)], hz.at[1], {"vert": below})
        remote(name, field.at[pl.ds(SUB * z, SUB)], hz.at[0], {"vert": above})
        for j in range(z):
            sx[0, pl.ds(j, 1), :] = field[pl.ds(SUB * (j + 1), 1), :]
            sx[1, pl.ds(j, 1), :] = field[pl.ds(SUB * (j + 2) - 1, 1), :]
        remote(name, sx.at[0], hx.at[1], {"plane": left})
        remote(name, sx.at[1], hx.at[0], {"plane": right})

    def side(name, value):
        m["sx_" + name][...] = value
        remote(name, m["sx_" + name], m["hx_" + name].at[1], {"plane": left})
        remote(name, m["sx_" + name], m["hx_" + name].at[0], {"plane": right})

    def gather(name, two):
        at = 2 * lax.rem(q, peers // 2)
        tile = jnp.where(sub == at, two[0], jnp.where(sub == at + 1, two[1], 0.0))
        slot = pl.ds(pl.multiple_of(q * SUB, SUB), SUB)
        m["own_" + name][...] = tile
        for step in range(1, peers):
            remote(name, m["own_" + name], m["all_" + name].at[slot], {"vert": lax.rem(q + step, peers)})
        m["all_" + name][slot, :] = tile

    def column(name):
        arrive(name)
        parts = [m["all_" + name][pl.ds(SUB * i, SUB), :] for i in range(peers)]
        half = peers // 2
        return jnp.concatenate([sum(parts[1:half], parts[0]), sum(parts[half + 1:], parts[half])], axis=0)

    def chunks(z, step):
        size = min(CHUNK, z)
        if z == size:
            step(0, size)
        else:
            def run(i, carry):
                step(i * size, size)
                return carry
            lax.fori_loop(0, z // size, run, 0)

    def rows(z, size):
        start = SUB * z
        if not isinstance(z, int):
            start = pl.multiple_of(start, SUB)
        return pl.ds(start, SUB * size)

    def get(name, z, size):
        return m[name][rows(z, size), :].reshape(size, SUB, lanes)

    def put(name, z, size, value):
        m[name][rows(z, size), :] = value.reshape(size * SUB, lanes)

    def restrict(value, k):
        s = 1 << k
        n = value.shape[0]
        value = value.reshape(n // 2, 2, SUB, lanes)
        value = value[:, 0] + value[:, 1]
        value = value + jnp.where((lane & s) != 0, pltpu.roll(value, s, 2), pltpu.roll(value, lanes - s, 2))
        other = pltpu.roll(value, s, 1)
        if 2 * s != SUB:
            other = jnp.where((sub & s) != 0, other, pltpu.roll(value, SUB - s, 1))
        return value + other

    def edge_rows(name, z, size):
        hx = m["hx_" + name]
        result = []
        for j in range(size):
            lo = jnp.broadcast_to(hx[0, pl.ds(z + j, 1), :], (SUB, lanes))
            hi = jnp.broadcast_to(hx[1, pl.ds(z + j, 1), :], (SUB, lanes))
            result.append(jnp.where(sub < SUB // 2, lo, hi))
        return jnp.stack(result)

    def coefficients(k):
        s = 1 << k
        z_all = depth >> k
        name = "b" + str(k)
        arrive(name)
        m[name][rows(0, 1), :] = m["hz_" + name][0] * q_lo
        m[name][rows(z_all + 1, 1), :] = m["hz_" + name][1] * q_hi
        edge = jnp.where(sub < SUB // 2, p_lo, p_hi)
        outer = jnp.logical_or(sub < s, sub >= SUB - s)

        def step(z, size):
            b = 0.5 * get(name, z + 1, size)
            zm = b + 0.5 * get(name, z, size)
            zp = b + 0.5 * get(name, z + 2, size)
            xe = b + 0.5 * (edge_rows(name, z, size) * edge)
            ym_in = jnp.where(lane < s, 0.0, b + pltpu.roll(b, s, 2))
            yp_in = jnp.where(lane >= lanes - s, 0.0, b + pltpu.roll(b, lanes - s, 2))
            xm_in = jnp.where(sub < s, 0.0, b + pltpu.roll(b, s, 1))
            xp_in = jnp.where(sub >= SUB - s, 0.0, b + pltpu.roll(b, SUB - s, 1))
            ch = jnp.where(outer, xe, 0.0)
            ends = jnp.where(jnp.logical_or(lane < s, lane >= lanes - s), b, 0.0)
            diag = zm + zp + ym_in + yp_in + xm_in + xp_in + ch + ends
            k_ = str(k)
            put("cz" + k_, z, size, zm)
            put("cym" + k_, z, size, ym_in)
            put("cyp" + k_, z, size, yp_in)
            put("cxm" + k_, z, size, xm_in)
            put("cxp" + k_, z, size, xp_in)
            put("ch" + k_, z, size, ch * edge)
            put("d" + k_, z, size, diag)
            put("w" + k_, z, size, RELAX_WEIGHT / diag)

        chunks(z_all, step)
        last = 0.5 * m[name][rows(z_all, 1), :] + 0.5 * m[name][rows(z_all + 1, 1), :]
        m["cz" + str(k)][rows(z_all, 1), :] = last * q_hi
        m["cz" + str(k)][rows(0, 1), :] = m["cz" + str(k)][rows(0, 1), :] * q_lo

    def inner_terms(k, name):
        s = 1 << k
        k_ = str(k)

        def step(z, size):
            v = get(name, z + 1, size)
            t = get("g" + k_, z, size)
            t = t + get("cz" + k_, z, size) * get(name, z, size)
            t = t + get("cz" + k_, z + 1, size) * get(name, z + 2, size)
            t = t + get("cym" + k_, z, size) * pltpu.roll(v, s, 2)
            t = t + get("cyp" + k_, z, size) * pltpu.roll(v, lanes - s, 2)
            t = t + get("cxm" + k_, z, size) * pltpu.roll(v, s, 1)
            t = t + get("cxp" + k_, z, size) * pltpu.roll(v, SUB - s, 1)
            put("t" + k_, z, size, t)

        chunks(depth >> k, step)

    def with_halo(k, name, use):
        z_all = depth >> k
        k_ = str(k)
        t, cz, hz = m["t" + k_], m["cz" + k_], m["hz_" + name]
        arrive(name)
        t[rows(0, 1), :] = t[rows(0, 1), :] + cz[rows(0, 1), :] * hz[0]
        t[rows(z_all - 1, 1), :] = t[rows(z_all - 1, 1), :] + cz[rows(z_all, 1), :] * hz[1]

        def step(z, size):
            use(z, size, get("t" + k_, z, size) + get("ch" + k_, z, size) * edge_rows(name, z, size))

        chunks(z_all, step)

    def relaxed(k, name, store):
        k_ = str(k)

        def use(z, size, total):
            store(z, size, KEEP * get(name, z + 1, size) + get("w" + k_, z, size) * total)

        with_halo(k, name, use)

    loads[0].wait()
    loads[1].wait()
    pl.semaphore_wait(barrier, peers + 1)
    exchange("b0", m["b0"])
    exchange("vin", m["vin"])
    for k in range(2):
        def coarser(z, size, k=k):
            half = z // 2
            put("b" + str(k + 1), half + 1, size // 2, 0.125 * restrict(get("b" + str(k), z + 1, size), k))
        chunks(depth >> k, coarser)
        exchange("b" + str(k + 1), m["b" + str(k + 1)])
    gather("gb", 0.125 * restrict(get("b2", 1, depth >> 2), 2))

    coefficients(0)
    loads[2].wait()
    inner_terms(0, "vin")
    relaxed(0, "vin", lambda z, size, value: put("v0", z + 1, size, value))
    exchange("v0", m["v0"])
    inner_terms(0, "v0")
    coefficients(1)
    bc = column("gb")
    side("bc", bc)

    def down(k, name):
        k_, n_ = str(k), str(k + 1)

        def use(z, size, total):
            r = total - get("d" + k_, z, size) * get(name, z + 1, size)
            g = 0.5 * restrict(r, k)
            if k == 2:
                gather("gf", g)
                return
            half = z // 2
            put("g" + n_, half, size // 2, g)
            put("v" + n_, half + 1, size // 2, g * get("w" + n_, half, size // 2))

        with_halo(k, name, use)

    down(0, "v0")
    exchange("v1", m["v1"])
    inner_terms(1, "v1")
    coefficients(2)
    down(1, "v1")
    exchange("v2", m["v2"])
    inner_terms(2, "v2")

    size_y = 1 << 3
    tall = 2 * peers
    lane_c = lax.broadcasted_iota(jnp.int32, (tall, lanes), 1)
    row_c = lax.broadcasted_iota(jnp.int32, (tall, lanes), 0)
    arrive("bc")
    b = 0.5 * bc
    xm = b + (0.5 * p_lo) * m["hx_bc"][0]
    xp = b + (0.5 * p_hi) * m["hx_bc"][1]
    y_lo, y_hi = lane_c < size_y, lane_c >= lanes - size_y
    z_lo, z_hi = row_c == 0, row_c == tall - 1
    ym = b + jnp.where(y_lo, 0.0, pltpu.roll(b, size_y, 1))
    yp = b + jnp.where(y_hi, 0.0, pltpu.roll(b, lanes - size_y, 1))
    zm = b + jnp.where(z_lo, 0.0, pltpu.roll(b, 1, 0))
    zp = b + jnp.where(z_hi, 0.0, pltpu.roll(b, tall - 1, 0))
    diag = xm + xp + ym + yp + zm + zp
    weight = RELAX_WEIGHT / diag
    diag_total = jnp.sum(diag, axis=0, keepdims=True)
    xm, xp = xm * p_lo, xp * p_hi
    ym, yp = jnp.where(y_lo, 0.0, ym), jnp.where(y_hi, 0.0, yp)
    zm, zp = jnp.where(z_lo, 0.0, zm), jnp.where(z_hi, 0.0, zp)

    down(2, "v2")
    forcing = column("gf")
    guess = weight * forcing

    for sweep in range(COARSE_SWEEPS):
        name = "s" + str(sweep)
        side(name, guess)
        total = (forcing + ym * pltpu.roll(guess, size_y, 1) + yp * pltpu.roll(guess, lanes - size_y, 1)
                 + zm * pltpu.roll(guess, 1, 0) + zp * pltpu.roll(guess, tall - 1, 0))
        arrive(name)
        total = total + xm * m["hx_" + name][0] + xp * m["hx_" + name][1]
        if sweep < COARSE_SWEEPS - 1:
            guess = KEEP * guess + weight * total
    res_total = jnp.sum(total - diag * guess, axis=0, keepdims=True)
    m["col"][...] = guess + RELAX_WEIGHT * res_total / diag_total

    own = [jnp.broadcast_to(m["col"][pl.ds(2 * q + j, 1), :], (SUB, lanes)) for j in range(2)]

    for j in range(depth >> 2):
        m["u2"][rows(j + 1, 1), :] = m["v2"][rows(j + 1, 1), :] + own[j // 2]
    exchange("u2", m["u2"])
    inner_terms(2, "u2")
    relaxed(2, "u2", lambda z, size, value: put("r2", z, size, value))

    def add_coarse(k):
        fine, coarse, result = "v" + str(k), "r" + str(k + 1), "u" + str(k)

        def step(z, size):
            half = z // 2
            c = get(coarse, half, size // 2)
            c = jnp.stack([c[i // 2] for i in range(size)])
            put(result, z + 1, size, get(fine, z + 1, size) + c)

        chunks(depth >> k, step)

    add_coarse(1)
    exchange("u1", m["u1"])
    inner_terms(1, "u1")
    relaxed(1, "u1", lambda z, size, value: put("r1", z, size, value))

    add_coarse(0)
    exchange("u0", m["u0"])
    inner_terms(0, "u0")

    def store(z, size, value):
        out[rows(z, size), :] = value.reshape(size * SUB, lanes)

    relaxed(0, "u0", store)
    for copy in started:
        copy.wait_send()


def local(planes, peers, source, density, pressure):
    depth, width, lanes = source.shape
    flat = lambda x: x.reshape(depth * width, lanes)
    plan = scratch_plan(depth, lanes, peers)
    call = pl.pallas_call(
        functools.partial(cycle_kernel, tuple(plan), depth, lanes, planes, peers),
        out_shape=jax.ShapeDtypeStruct((depth * width, lanes), jnp.float32),
        in_specs=[pl.BlockSpec(memory_space=pl.ANY)] * 3,
        out_specs=pl.BlockSpec(memory_space=pltpu.VMEM),
        scratch_shapes=list(plan.values()),
        compiler_params=pltpu.CompilerParams(collective_id=0, has_side_effects=True),
        name="v_cycle",
    )
    return call(flat(source), flat(density), flat(pressure)).reshape(depth, width, lanes)


def solution(mesh):
    spec = P("vert", "plane", None)
    body = functools.partial(local, mesh.shape["plane"], mesh.shape["vert"])
    return jax.shard_map(body, mesh=mesh, in_specs=(spec, spec, spec), out_specs=spec, check_vma=False)
```

time: 313 us -> 79.6 us (0.25)
  the two profiles are of different devices: /device:TPU:7 before, /device:TPU:1 now
where the time goes in v1:
time: 79.6 us; the launch traced here: 79.4 us
  Pallas kernels  77.8 us (98%)
  local copies, waits for them, and re-layouts  1.67 us (2%)
    pallas_call x1, Pallas kernels, local(): call(flat(source), flat(density), flat(pressure))  77.8 us
    unnamed x1, local copies, waits for them, and re-layouts  1.67 us

profile of v1, /device:TPU:1, one launch (start us, length us, event | category | flops | bytes accessed | tf_op | source)
XLA Modules:
  0.0 79.4 jit_solution(6364571665568445607)
XLA Ops:
  0.0 77.8 %v_cycle.1 = f32[128,512]{1,0:T(8,128)} custom-call(f32[128,512]{1,0:T(8,128)} %bitcast.5, f32[128,512]{1,0:T(8,128)} %bitcast.6, f32[128,512]{1,0:T(8,128)} %bitcast.7), custom_call_target="tpu_custom_call" | custom-call | tf_op jit(solution)/shard_map/v_cycle/pallas_call | solution.py:386
  77.8 1.7 %copy.5 = f32[16,8,512]{2,1,0:T(8,128)} copy(f32[16,8,512]{2,1,0:T(8,128)} %bitcast.4) | data formatting | bytes 524288

commit v2 on v1

--- a/solution.py
+++ b/solution.py
@@ -13,10 +13,11 @@
 MESH = pl.DeviceIdType.MESH
 CHUNK = 4
 SUB = 8
+NARROW = 128
 
 EXCHANGES = ("vin", "b0", "b1", "b2", "v0", "v1", "v2", "u2", "u1", "u0")
 LEVEL_OF = {"vin": 0, "b0": 0, "b1": 1, "b2": 2, "v0": 0, "v1": 1, "v2": 2, "u2": 2, "u1": 1, "u0": 0}
-SIDES = ("bc", "s0", "s1", "s2", "s3")
+SIDES = {"bc": COARSE_SWEEPS + 1, "fc": COARSE_SWEEPS}
 GATHERS = ("gb", "gf")
 
 
@@ -37,16 +38,16 @@
         plan["sx_" + name] = pltpu.VMEM((2, z, lanes), jnp.float32)
         plan["hz_" + name] = pltpu.VMEM((2, SUB, lanes), jnp.float32)
     column = 2 * peers
-    for name in SIDES:
-        plan["hx_" + name] = pltpu.VMEM((2, column, lanes), jnp.float32)
-        plan["sx_" + name] = pltpu.VMEM((column, lanes), jnp.float32)
+    for name, reach in SIDES.items():
+        plan["hx_" + name] = pltpu.VMEM((2 * reach + 1, column, NARROW), jnp.float32)
+        plan["sx_" + name] = pltpu.VMEM((column, NARROW), jnp.float32)
     for name in GATHERS:
-        plan["all_" + name] = pltpu.VMEM((peers * SUB, lanes), jnp.float32)
-        plan["own_" + name] = pltpu.VMEM((SUB, lanes), jnp.float32)
+        plan["all_" + name] = pltpu.VMEM((peers * SUB, NARROW), jnp.float32)
+        plan["own_" + name] = pltpu.VMEM((SUB, NARROW), jnp.float32)
     plan["r2"] = field(depth >> 2)
     plan["r1"] = field(depth >> 1)
-    plan["col"] = pltpu.VMEM((column, lanes), jnp.float32)
-    count = 4 * len(EXCHANGES) + 2 * len(SIDES) + (peers - 1) * len(GATHERS)
+    plan["col"] = pltpu.VMEM((column, NARROW), jnp.float32)
+    count = 4 * len(EXCHANGES) + 2 * sum(SIDES.values()) + (peers - 1) * len(GATHERS)
     plan["send"] = pltpu.SemaphoreType.DMA((count,))
     plan["recv"] = pltpu.SemaphoreType.DMA((count,))
     plan["load"] = pltpu.SemaphoreType.DMA((3,))
@@ -58,10 +59,8 @@
     p, q = lax.axis_index("plane"), lax.axis_index("vert")
     left, right = lax.rem(p + planes - 1, planes), lax.rem(p + 1, planes)
     below, above = lax.rem(q + peers - 1, peers), lax.rem(q + 1, peers)
-    p_lo = jnp.where(p == 0, 0.0, 1.0).astype(jnp.float32)
-    p_hi = jnp.where(p == planes - 1, 0.0, 1.0).astype(jnp.float32)
-    q_lo = jnp.where(q == 0, 0.0, 1.0).astype(jnp.float32)
-    q_hi = jnp.where(q == peers - 1, 0.0, 1.0).astype(jnp.float32)
+    has_left, has_right, has_below, has_above = p > 0, p < planes - 1, q > 0, q < peers - 1
+    far = SIDES["bc"]
 
     loads = []
     for i, (src, dst) in enumerate(((density, m["b0"].at[pl.ds(SUB, SUB * depth)]),
@@ -71,8 +70,14 @@
         loads[-1].start()
 
     barrier = pltpu.get_barrier_semaphore()
-    for peer in (left, right):
-        pl.semaphore_signal(barrier, inc=1, device_id={"plane": peer}, device_id_type=MESH)
+    for step in range(1, far + 1):
+        @pl.when(p >= step)
+        def _(step=step):
+            pl.semaphore_signal(barrier, inc=1, device_id={"plane": p - step}, device_id_type=MESH)
+
+        @pl.when(p + step < planes)
+        def _(step=step):
+            pl.semaphore_signal(barrier, inc=1, device_id={"plane": p + step}, device_id_type=MESH)
     for step in range(1, peers):
         pl.semaphore_signal(barrier, inc=1, device_id={"vert": lax.rem(q + step, peers)}, device_id_type=MESH)
 
@@ -82,6 +87,19 @@
         m[name][pl.ds(0, SUB), :] = zero
         m[name][pl.ds(SUB * (z + 1), SUB), :] = zero
 
+    for name in EXCHANGES:
+        for absent, half, slot in ((p == 0, "hx_", 0), (p == planes - 1, "hx_", 1),
+                                   (q == 0, "hz_", 0), (q == peers - 1, "hz_", 1)):
+            @pl.when(absent)
+            def _(ref=m[half + name], slot=slot):
+                ref[slot] = jnp.zeros(ref.shape[1:], jnp.float32)
+    for name, reach in SIDES.items():
+        for step in range(1, reach + 1):
+            for absent, slot in ((p < step, reach - step), (p + step >= planes, reach + step)):
+                @pl.when(absent)
+                def _(ref=m["hx_" + name], slot=slot):
+                    ref[slot] = jnp.zeros(ref.shape[1:], jnp.float32)
+
     lane = lax.broadcasted_iota(jnp.int32, (SUB, lanes), 1)
     sub = lax.broadcasted_iota(jnp.int32, (SUB, lanes), 0)
 
@@ -89,39 +107,63 @@
     pending = {}
     started = []
 
-    def remote(key, src, dst, device):
+    def only(condition, action):
+        if condition is None:
+            action()
+        else:
+            pl.when(condition)(action)
+
+    def remote(key, src, dst, device, sends=None, receives=None):
         at = used[0]
         used[0] += 1
         copy = pltpu.make_async_remote_copy(
             src_ref=src, dst_ref=dst, send_sem=m["send"].at[at], recv_sem=m["recv"].at[at],
             device_id=device, device_id_type=MESH)
-        copy.start()
-        pending.setdefault(key, []).append(copy)
-        started.append(copy)
+        only(sends, lambda: copy.start())
+        pending.setdefault(key, []).append((copy, receives))
+        started.append((copy, sends))
 
     def arrive(key):
-        for copy in pending.pop(key):
-            copy.wait_recv()
+        for copy, receives in pending.pop(key):
+            only(receives, lambda copy=copy: copy.wait_recv())
 
     def exchange(name, field):
         z = depth >> LEVEL_OF[name]
         hx, sx, hz = m["hx_" + name], m["sx_" + name], m["hz_" + name]
-        remote(name, field.at[pl.ds(SUB, SUB)], hz.at[1], {"vert": below})
-        remote(name, field.at[pl.ds(SUB * z, SUB)], hz.at[0], {"vert": above})
+        remote(name, field.at[pl.ds(SUB, SUB)], hz.at[1], {"vert": below}, has_below, has_above)
+        remote(name, field.at[pl.ds(SUB * z, SUB)], hz.at[0], {"vert": above}, has_above, has_below)
         for j in range(z):
             sx[0, pl.ds(j, 1), :] = field[pl.ds(SUB * (j + 1), 1), :]
             sx[1, pl.ds(j, 1), :] = field[pl.ds(SUB * (j + 2) - 1, 1), :]
-        remote(name, sx.at[0], hx.at[1], {"plane": left})
-        remote(name, sx.at[1], hx.at[0], {"plane": right})
+        remote(name, sx.at[0], hx.at[1], {"plane": left}, has_left, has_right)
+        remote(name, sx.at[1], hx.at[0], {"plane": right}, has_right, has_left)
 
     def side(name, value):
-        m["sx_" + name][...] = value
-        remote(name, m["sx_" + name], m["hx_" + name].at[1], {"plane": left})
-        remote(name, m["sx_" + name], m["hx_" + name].at[0], {"plane": right})
+        reach = SIDES[name]
+        sx, hx = m["sx_" + name], m["hx_" + name]
+        sx[...] = value
+        for step in range(1, reach + 1):
+            lower, upper = lax.rem(p + planes - step, planes), lax.rem(p + step, planes)
+            down, up = p >= step, p + step < planes
+            remote(name, sx, hx.at[reach + step], {"plane": lower}, down, up)
+            remote(name, sx, hx.at[reach - step], {"plane": upper}, up, down)
+
+    quarter = lax.broadcasted_iota(jnp.int32, (SUB, NARROW), 1) & 3
+
+    def narrow(tile):
+        parts = [tile[:, NARROW * j:NARROW * (j + 1)] for j in range(lanes // NARROW)]
+        return jnp.where(quarter == 0, parts[0], jnp.where(quarter == 1, parts[1],
+                         jnp.where(quarter == 2, parts[2], parts[3])))
+
+    def widen(tile):
+        moved = {d: pltpu.roll(tile, (NARROW - d) % NARROW, 1) if d else tile for d in range(-3, 4)}
+        return jnp.concatenate(
+            [jnp.where(quarter == 0, moved[j], jnp.where(quarter == 1, moved[j - 1],
+                       jnp.where(quarter == 2, moved[j - 2], moved[j - 3]))) for j in range(4)], axis=1)
 
     def gather(name, two):
         at = 2 * lax.rem(q, peers // 2)
-        tile = jnp.where(sub == at, two[0], jnp.where(sub == at + 1, two[1], 0.0))
+        tile = narrow(jnp.where(sub == at, two[0], jnp.where(sub == at + 1, two[1], 0.0)))
         slot = pl.ds(pl.multiple_of(q * SUB, SUB), SUB)
         m["own_" + name][...] = tile
         for step in range(1, peers):
@@ -181,16 +223,15 @@
         z_all = depth >> k
         name = "b" + str(k)
         arrive(name)
-        m[name][rows(0, 1), :] = m["hz_" + name][0] * q_lo
-        m[name][rows(z_all + 1, 1), :] = m["hz_" + name][1] * q_hi
-        edge = jnp.where(sub < SUB // 2, p_lo, p_hi)
+        m[name][rows(0, 1), :] = m["hz_" + name][0]
+        m[name][rows(z_all + 1, 1), :] = m["hz_" + name][1]
         outer = jnp.logical_or(sub < s, sub >= SUB - s)
 
         def step(z, size):
             b = 0.5 * get(name, z + 1, size)
             zm = b + 0.5 * get(name, z, size)
             zp = b + 0.5 * get(name, z + 2, size)
-            xe = b + 0.5 * (edge_rows(name, z, size) * edge)
+            xe = b + 0.5 * edge_rows(name, z, size)
             ym_in = jnp.where(lane < s, 0.0, b + pltpu.roll(b, s, 2))
             yp_in = jnp.where(lane >= lanes - s, 0.0, b + pltpu.roll(b, lanes - s, 2))
             xm_in = jnp.where(sub < s, 0.0, b + pltpu.roll(b, s, 1))
@@ -204,14 +245,13 @@
             put("cyp" + k_, z, size, yp_in)
             put("cxm" + k_, z, size, xm_in)
             put("cxp" + k_, z, size, xp_in)
-            put("ch" + k_, z, size, ch * edge)
+            put("ch" + k_, z, size, ch)
             put("d" + k_, z, size, diag)
             put("w" + k_, z, size, RELAX_WEIGHT / diag)
 
         chunks(z_all, step)
         last = 0.5 * m[name][rows(z_all, 1), :] + 0.5 * m[name][rows(z_all + 1, 1), :]
-        m["cz" + str(k)][rows(z_all, 1), :] = last * q_hi
-        m["cz" + str(k)][rows(0, 1), :] = m["cz" + str(k)][rows(0, 1), :] * q_lo
+        m["cz" + str(k)][rows(z_all, 1), :] = last
 
     def inner_terms(k, name):
         s = 1 << k
@@ -253,7 +293,8 @@
 
     loads[0].wait()
     loads[1].wait()
-    pl.semaphore_wait(barrier, peers + 1)
+    greeted = jnp.minimum(p, far) + jnp.minimum(planes - 1 - p, far) + peers - 1
+    pl.semaphore_wait(barrier, greeted)
     exchange("b0", m["b0"])
     exchange("vin", m["vin"])
     for k in range(2):
@@ -297,44 +338,59 @@
     exchange("v2", m["v2"])
     inner_terms(2, "v2")
 
-    size_y = 1 << 3
+    reach = COARSE_SWEEPS
     tall = 2 * peers
-    lane_c = lax.broadcasted_iota(jnp.int32, (tall, lanes), 1)
-    row_c = lax.broadcasted_iota(jnp.int32, (tall, lanes), 0)
+    lane_c = lax.broadcasted_iota(jnp.int32, (tall, NARROW), 1)
+    row_c = lax.broadcasted_iota(jnp.int32, (tall, NARROW), 0)
+    y_lo = jnp.logical_or(lane_c == 0, lane_c == 4)
+    y_hi = jnp.logical_or(lane_c == NARROW - 5, lane_c == NARROW - 1)
+    z_lo, z_hi = row_c == 0, row_c == tall - 1
+
+    def before_y(v):
+        return jnp.where(lane_c < 8, pltpu.roll(v, 9, 1), pltpu.roll(v, 8, 1))
+
+    def after_y(v):
+        return jnp.where(lane_c >= NARROW - 8, pltpu.roll(v, NARROW - 9, 1), pltpu.roll(v, NARROW - 8, 1))
+
     arrive("bc")
-    b = 0.5 * bc
-    xm = b + (0.5 * p_lo) * m["hx_bc"][0]
-    xp = b + (0.5 * p_hi) * m["hx_bc"][1]
-    y_lo, y_hi = lane_c < size_y, lane_c >= lanes - size_y
-    z_lo, z_hi = row_c == 0, row_c == tall - 1
-    ym = b + jnp.where(y_lo, 0.0, pltpu.roll(b, size_y, 1))
-    yp = b + jnp.where(y_hi, 0.0, pltpu.roll(b, lanes - size_y, 1))
-    zm = b + jnp.where(z_lo, 0.0, pltpu.roll(b, 1, 0))
-    zp = b + jnp.where(z_hi, 0.0, pltpu.roll(b, tall - 1, 0))
-    diag = xm + xp + ym + yp + zm + zp
-    weight = RELAX_WEIGHT / diag
-    diag_total = jnp.sum(diag, axis=0, keepdims=True)
-    xm, xp = xm * p_lo, xp * p_hi
-    ym, yp = jnp.where(y_lo, 0.0, ym), jnp.where(y_hi, 0.0, yp)
-    zm, zp = jnp.where(z_lo, 0.0, zm), jnp.where(z_hi, 0.0, zp)
+    b = {o: 0.5 * (bc if o == 0 else m["hx_bc"][far + o]) for o in range(-far, far + 1)}
+    xp = {o: b[o] + b[o + 1] for o in range(-far, far)}
+    ym, yp, zm, zp, weight = {}, {}, {}, {}, {}
+    for o in range(-reach, reach + 1):
+        ym[o] = b[o] + jnp.where(y_lo, 0.0, before_y(b[o]))
+        yp[o] = b[o] + jnp.where(y_hi, 0.0, after_y(b[o]))
+        zm[o] = b[o] + jnp.where(z_lo, 0.0, pltpu.roll(b[o], 1, 0))
+        zp[o] = b[o] + jnp.where(z_hi, 0.0, pltpu.roll(b[o], tall - 1, 0))
+        diag = xp[o - 1] + xp[o] + ym[o] + yp[o] + zm[o] + zp[o]
+        if o == 0:
+            diag_own = diag
+            weight[o] = RELAX_WEIGHT / diag
+        else:
+            inside = jnp.where(jnp.logical_and(p + o >= 0, p + o < planes), 1.0, 0.0).astype(jnp.float32)
+            weight[o] = (RELAX_WEIGHT * inside) / (diag + (1.0 - inside))
+        ym[o], yp[o] = jnp.where(y_lo, 0.0, ym[o]), jnp.where(y_hi, 0.0, yp[o])
+        zm[o], zp[o] = jnp.where(z_lo, 0.0, zm[o]), jnp.where(z_hi, 0.0, zp[o])
+    diag_total = jnp.sum(diag_own, axis=0, keepdims=True)
 
     down(2, "v2")
-    forcing = column("gf")
-    guess = weight * forcing
-
-    for sweep in range(COARSE_SWEEPS):
-        name = "s" + str(sweep)
-        side(name, guess)
-        total = (forcing + ym * pltpu.roll(guess, size_y, 1) + yp * pltpu.roll(guess, lanes - size_y, 1)
-                 + zm * pltpu.roll(guess, 1, 0) + zp * pltpu.roll(guess, tall - 1, 0))
-        arrive(name)
-        total = total + xm * m["hx_" + name][0] + xp * m["hx_" + name][1]
-        if sweep < COARSE_SWEEPS - 1:
-            guess = KEEP * guess + weight * total
-    res_total = jnp.sum(total - diag * guess, axis=0, keepdims=True)
-    m["col"][...] = guess + RELAX_WEIGHT * res_total / diag_total
-
-    own = [jnp.broadcast_to(m["col"][pl.ds(2 * q + j, 1), :], (SUB, lanes)) for j in range(2)]
+    own_forcing = column("gf")
+    side("fc", own_forcing)
+    arrive("fc")
+    forcing = {o: own_forcing if o == 0 else m["hx_fc"][reach + o] for o in range(-reach, reach + 1)}
+    guess = {o: weight[o] * forcing[o] for o in forcing}
+
+    def total_of(o):
+        v = guess[o]
+        return (forcing[o] + xp[o - 1] * guess[o - 1] + xp[o] * guess[o + 1]
+                + ym[o] * before_y(v) + yp[o] * after_y(v)
+                + zm[o] * pltpu.roll(v, 1, 0) + zp[o] * pltpu.roll(v, tall - 1, 0))
+
+    for wide in range(COARSE_SWEEPS - 1, 0, -1):
+        guess = {o: KEEP * guess[o] + weight[o] * total_of(o) for o in range(-wide, wide + 1)}
+    res_total = jnp.sum(total_of(0) - diag_own * guess[0], axis=0, keepdims=True)
+    m["col"][...] = guess[0] + RELAX_WEIGHT * res_total / diag_total
+
+    own = [widen(jnp.broadcast_to(m["col"][pl.ds(2 * q + j, 1), :], (SUB, NARROW))) for j in range(2)]
 
     for j in range(depth >> 2):
         m["u2"][rows(j + 1, 1), :] = m["v2"][rows(j + 1, 1), :] + own[j // 2]
@@ -366,8 +422,8 @@
         out[rows(z, size), :] = value.reshape(size * SUB, lanes)
 
     relaxed(0, "u0", store)
-    for copy in started:
-        copy.wait_send()
+    for copy, sends in started:
+        only(sends, lambda copy=copy: copy.wait_send())
 
 
 def local(planes, peers, source, density, pressure):

time: 79.6 us -> 60.5 us (0.76)
  the two profiles are of different devices: /device:TPU:1 before, /device:TPU:4 now
where the time goes in v2:
time: 60.5 us; the launch traced here: 60.3 us
  Pallas kernels  58.7 us (97%)
  local copies, waits for them, and re-layouts  1.67 us (3%)
    pallas_call x1, Pallas kernels, local(): call(flat(source), flat(density), flat(pressure))  58.7 us
    unnamed x1, local copies, waits for them, and re-layouts  1.67 us

profile of v2, /device:TPU:4, one launch (start us, length us, event | category | flops | bytes accessed | tf_op | source)
XLA Modules:
  0.0 60.3 jit_solution(15667405732456533831)
XLA Ops:
  0.0 58.7 %v_cycle.1 = f32[128,512]{1,0:T(8,128)} custom-call(f32[128,512]{1,0:T(8,128)} %bitcast.5, f32[128,512]{1,0:T(8,128)} %bitcast.6, f32[128,512]{1,0:T(8,128)} %bitcast.7), custom_call_target="tpu_custom_call" | custom-call | tf_op jit(solution)/shard_map/v_cycle/pallas_call | solution.py:442
  58.7 1.7 %copy.5 = f32[16,8,512]{2,1,0:T(8,128)} copy(f32[16,8,512]{2,1,0:T(8,128)} %bitcast.4) | data formatting | bytes 524288

commit v3 on v2

--- a/solution.py
+++ b/solution.py
@@ -17,7 +17,7 @@
 
 EXCHANGES = ("vin", "b0", "b1", "b2", "v0", "v1", "v2", "u2", "u1", "u0")
 LEVEL_OF = {"vin": 0, "b0": 0, "b1": 1, "b2": 2, "v0": 0, "v1": 1, "v2": 2, "u2": 2, "u1": 1, "u0": 0}
-SIDES = {"bc": COARSE_SWEEPS + 1, "fc": COARSE_SWEEPS}
+SIDES = {"bc": COARSE_SWEEPS + 2, "fc": COARSE_SWEEPS + 1}
 GATHERS = ("gb", "gf")
 
 
@@ -46,7 +46,9 @@
         plan["own_" + name] = pltpu.VMEM((SUB, NARROW), jnp.float32)
     plan["r2"] = field(depth >> 2)
     plan["r1"] = field(depth >> 1)
-    plan["col"] = pltpu.VMEM((column, NARROW), jnp.float32)
+    plan["col"] = pltpu.VMEM((3, column + 2 * SUB, NARROW), jnp.float32)
+    plan["pick"] = pltpu.VMEM((SUB, NARROW), jnp.float32)
+    plan["wide"] = pltpu.VMEM((SUB, lanes), jnp.float32)
     count = 4 * len(EXCHANGES) + 2 * sum(SIDES.values()) + (peers - 1) * len(GATHERS)
     plan["send"] = pltpu.SemaphoreType.DMA((count,))
     plan["recv"] = pltpu.SemaphoreType.DMA((count,))
@@ -124,19 +126,19 @@
         started.append((copy, sends))
 
     def arrive(key):
-        for copy, receives in pending.pop(key):
+        for copy, receives in pending.pop(key, ()):
             only(receives, lambda copy=copy: copy.wait_recv())
 
     def exchange(name, field):
         z = depth >> LEVEL_OF[name]
         hx, sx, hz = m["hx_" + name], m["sx_" + name], m["hz_" + name]
-        remote(name, field.at[pl.ds(SUB, SUB)], hz.at[1], {"vert": below}, has_below, has_above)
-        remote(name, field.at[pl.ds(SUB * z, SUB)], hz.at[0], {"vert": above}, has_above, has_below)
         for j in range(z):
             sx[0, pl.ds(j, 1), :] = field[pl.ds(SUB * (j + 1), 1), :]
             sx[1, pl.ds(j, 1), :] = field[pl.ds(SUB * (j + 2) - 1, 1), :]
         remote(name, sx.at[0], hx.at[1], {"plane": left}, has_left, has_right)
         remote(name, sx.at[1], hx.at[0], {"plane": right}, has_right, has_left)
+        remote(name, field.at[pl.ds(SUB, SUB)], hz.at[1], {"vert": below}, has_below, has_above)
+        remote(name, field.at[pl.ds(SUB * z, SUB)], hz.at[0], {"vert": above}, has_above, has_below)
 
     def side(name, value):
         reach = SIDES[name]
@@ -184,7 +186,7 @@
             def run(i, carry):
                 step(i * size, size)
                 return carry
-            lax.fori_loop(0, z // size, run, 0)
+            lax.fori_loop(0, z // size, run, 0, unroll=True)
 
     def rows(z, size):
         start = SUB * z
@@ -338,7 +340,7 @@
     exchange("v2", m["v2"])
     inner_terms(2, "v2")
 
-    reach = COARSE_SWEEPS
+    reach = COARSE_SWEEPS + 1
     tall = 2 * peers
     lane_c = lax.broadcasted_iota(jnp.int32, (tall, NARROW), 1)
     row_c = lax.broadcasted_iota(jnp.int32, (tall, NARROW), 0)
@@ -355,22 +357,22 @@
     arrive("bc")
     b = {o: 0.5 * (bc if o == 0 else m["hx_bc"][far + o]) for o in range(-far, far + 1)}
     xp = {o: b[o] + b[o + 1] for o in range(-far, far)}
-    ym, yp, zm, zp, weight = {}, {}, {}, {}, {}
+    ym, yp, zm, zp, diag, weight, inside = {}, {}, {}, {}, {}, {}, {}
     for o in range(-reach, reach + 1):
         ym[o] = b[o] + jnp.where(y_lo, 0.0, before_y(b[o]))
         yp[o] = b[o] + jnp.where(y_hi, 0.0, after_y(b[o]))
         zm[o] = b[o] + jnp.where(z_lo, 0.0, pltpu.roll(b[o], 1, 0))
         zp[o] = b[o] + jnp.where(z_hi, 0.0, pltpu.roll(b[o], tall - 1, 0))
-        diag = xp[o - 1] + xp[o] + ym[o] + yp[o] + zm[o] + zp[o]
-        if o == 0:
-            diag_own = diag
-            weight[o] = RELAX_WEIGHT / diag
-        else:
-            inside = jnp.where(jnp.logical_and(p + o >= 0, p + o < planes), 1.0, 0.0).astype(jnp.float32)
-            weight[o] = (RELAX_WEIGHT * inside) / (diag + (1.0 - inside))
+        diag[o] = xp[o - 1] + xp[o] + ym[o] + yp[o] + zm[o] + zp[o]
+        inside[o] = jnp.where(jnp.logical_and(p + o >= 0, p + o < planes), 1.0, 0.0).astype(jnp.float32)
+        weight[o] = (RELAX_WEIGHT * inside[o]) / (diag[o] + (1.0 - inside[o]))
         ym[o], yp[o] = jnp.where(y_lo, 0.0, ym[o]), jnp.where(y_hi, 0.0, yp[o])
         zm[o], zp[o] = jnp.where(z_lo, 0.0, zm[o]), jnp.where(z_hi, 0.0, zp[o])
-    diag_total = jnp.sum(diag_own, axis=0, keepdims=True)
+    share = {o: RELAX_WEIGHT * inside[o] / (jnp.sum(diag[o], axis=0, keepdims=True) + (1.0 - inside[o]))
+             for o in (-1, 0, 1)}
+    for o in range(3):
+        m["col"][o, pl.ds(0, SUB), :] = jnp.zeros((SUB, NARROW), jnp.float32)
+        m["col"][o, pl.ds(SUB + tall, SUB), :] = jnp.zeros((SUB, NARROW), jnp.float32)
 
     down(2, "v2")
     own_forcing = column("gf")
@@ -385,16 +387,26 @@
                 + ym[o] * before_y(v) + yp[o] * after_y(v)
                 + zm[o] * pltpu.roll(v, 1, 0) + zp[o] * pltpu.roll(v, tall - 1, 0))
 
-    for wide in range(COARSE_SWEEPS - 1, 0, -1):
+    for wide in range(COARSE_SWEEPS, 1, -1):
         guess = {o: KEEP * guess[o] + weight[o] * total_of(o) for o in range(-wide, wide + 1)}
-    res_total = jnp.sum(total_of(0) - diag_own * guess[0], axis=0, keepdims=True)
-    m["col"][...] = guess[0] + RELAX_WEIGHT * res_total / diag_total
-
-    own = [widen(jnp.broadcast_to(m["col"][pl.ds(2 * q + j, 1), :], (SUB, NARROW))) for j in range(2)]
-
+    for o in (-1, 0, 1):
+        res_total = jnp.sum(total_of(o) - diag[o] * guess[o], axis=0, keepdims=True)
+        m["col"][o + 1, pl.ds(SUB, tall), :] = guess[o] + share[o] * res_total
+
+    for i, (o, j) in enumerate(((0, -1), (0, 0), (0, 1), (0, 2), (-1, 0), (-1, 1), (1, 0), (1, 1))):
+        m["pick"][pl.ds(i, 1), :] = m["col"][o + 1, pl.ds(SUB + 2 * q + j, 1), :]
+    m["wide"][...] = widen(m["pick"][...])
+
+    def under(i):
+        return m["wide"][pl.ds(i, 1), :]
+
+    spread = lambda row: jnp.broadcast_to(row, (SUB, lanes))
     for j in range(depth >> 2):
-        m["u2"][rows(j + 1, 1), :] = m["v2"][rows(j + 1, 1), :] + own[j // 2]
-    exchange("u2", m["u2"])
+        m["u2"][rows(j + 1, 1), :] = m["v2"][rows(j + 1, 1), :] + spread(under(1 + j // 2))
+        m["hx_u2"][0, pl.ds(j, 1), :] = m["hx_v2"][0, pl.ds(j, 1), :] + under(4 + j // 2)
+        m["hx_u2"][1, pl.ds(j, 1), :] = m["hx_v2"][1, pl.ds(j, 1), :] + under(6 + j // 2)
+    m["hz_u2"][0] = m["hz_v2"][0] + spread(under(0))
+    m["hz_u2"][1] = m["hz_v2"][1] + spread(under(3))
     inner_terms(2, "u2")
     relaxed(2, "u2", lambda z, size, value: put("r2", z, size, value))
 

time: 60.5 us -> 55.7 us (0.921)
  the two profiles are of different devices: /device:TPU:4 before, /device:TPU:7 now
where the time goes in v3:
time: 55.7 us; the launch traced here: 55.4 us
  Pallas kernels  53.8 us (97%)
  local copies, waits for them, and re-layouts  1.67 us (3%)
    pallas_call x1, Pallas kernels, local(): call(flat(source), flat(density), flat(pressure))  53.8 us
    unnamed x1, local copies, waits for them, and re-layouts  1.67 us

profile of v3, /device:TPU:7, one launch (start us, length us, event | category | flops | bytes accessed | tf_op | source)
XLA Modules:
  0.0 55.4 jit_solution(1374902713277297590)
XLA Ops:
  0.0 53.8 %v_cycle.1 = f32[128,512]{1,0:T(8,128)} custom-call(f32[128,512]{1,0:T(8,128)} %bitcast.5, f32[128,512]{1,0:T(8,128)} %bitcast.6, f32[128,512]{1,0:T(8,128)} %bitcast.7), custom_call_target="tpu_custom_call" | custom-call | tf_op jit(solution)/shard_map/v_cycle/pallas_call | solution.py:454
  53.8 1.7 %copy.5 = f32[16,8,512]{2,1,0:T(8,128)} copy(f32[16,8,512]{2,1,0:T(8,128)} %bitcast.4) | data formatting | bytes 524288

commit v4 on v3

--- a/solution.py
+++ b/solution.py
@@ -39,8 +39,8 @@
         plan["hz_" + name] = pltpu.VMEM((2, SUB, lanes), jnp.float32)
     column = 2 * peers
     for name, reach in SIDES.items():
-        plan["hx_" + name] = pltpu.VMEM((2 * reach + 1, column, NARROW), jnp.float32)
-        plan["sx_" + name] = pltpu.VMEM((column, NARROW), jnp.float32)
+        plan["hx_" + name] = pltpu.VMEM((2 * reach + 1, SUB, NARROW), jnp.float32)
+        plan["sx_" + name] = pltpu.VMEM((SUB, NARROW), jnp.float32)
     for name in GATHERS:
         plan["all_" + name] = pltpu.VMEM((peers * SUB, NARROW), jnp.float32)
         plan["own_" + name] = pltpu.VMEM((SUB, NARROW), jnp.float32)
@@ -84,7 +84,7 @@
         pl.semaphore_signal(barrier, inc=1, device_id={"vert": lax.rem(q + step, peers)}, device_id_type=MESH)
 
     zero = jnp.zeros((SUB, lanes), jnp.float32)
-    for name in ("vin", "v0", "v1", "v2", "u0", "u1", "u2"):
+    for name in ("vin", "v0", "v1", "v2", "u0", "u1", "u2", "b0", "b1", "b2"):
         z = depth >> LEVEL_OF[name]
         m[name][pl.ds(0, SUB), :] = zero
         m[name][pl.ds(SUB * (z + 1), SUB), :] = zero
@@ -143,7 +143,7 @@
     def side(name, value):
         reach = SIDES[name]
         sx, hx = m["sx_" + name], m["hx_" + name]
-        sx[...] = value
+        sx[...] = jnp.where(twin, value[SUB:], value[:SUB])
         for step in range(1, reach + 1):
             lower, upper = lax.rem(p + planes - step, planes), lax.rem(p + step, planes)
             down, up = p >= step, p + step < planes
@@ -151,6 +151,13 @@
             remote(name, sx, hx.at[reach - step], {"plane": upper}, up, down)
 
     quarter = lax.broadcasted_iota(jnp.int32, (SUB, NARROW), 1) & 3
+
+    twin = (lax.broadcasted_iota(jnp.int32, (SUB, NARROW), 1) & 4) != 0
+
+    def side_column(name, offset):
+        both = m["hx_" + name][SIDES[name] + offset]
+        top = jnp.where(twin, pltpu.roll(both, 4, 1), both)
+        return jnp.concatenate([top, jnp.where(twin, both, pltpu.roll(both, NARROW - 4, 1))], axis=0)
 
     def narrow(tile):
         parts = [tile[:, NARROW * j:NARROW * (j + 1)] for j in range(lanes // NARROW)]
@@ -220,40 +227,51 @@
             result.append(jnp.where(sub < SUB // 2, lo, hi))
         return jnp.stack(result)
 
-    def coefficients(k):
+    def inner_coefficients(k):
         s = 1 << k
         z_all = depth >> k
-        name = "b" + str(k)
-        arrive(name)
-        m[name][rows(0, 1), :] = m["hz_" + name][0]
-        m[name][rows(z_all + 1, 1), :] = m["hz_" + name][1]
-        outer = jnp.logical_or(sub < s, sub >= SUB - s)
+        name, k_ = "b" + str(k), str(k)
+        ends_y = jnp.logical_or(lane < s, lane >= lanes - s)
 
         def step(z, size):
             b = 0.5 * get(name, z + 1, size)
             zm = b + 0.5 * get(name, z, size)
             zp = b + 0.5 * get(name, z + 2, size)
-            xe = b + 0.5 * edge_rows(name, z, size)
-            ym_in = jnp.where(lane < s, 0.0, b + pltpu.roll(b, s, 2))
-            yp_in = jnp.where(lane >= lanes - s, 0.0, b + pltpu.roll(b, lanes - s, 2))
-            xm_in = jnp.where(sub < s, 0.0, b + pltpu.roll(b, s, 1))
-            xp_in = jnp.where(sub >= SUB - s, 0.0, b + pltpu.roll(b, SUB - s, 1))
-            ch = jnp.where(outer, xe, 0.0)
-            ends = jnp.where(jnp.logical_or(lane < s, lane >= lanes - s), b, 0.0)
-            diag = zm + zp + ym_in + yp_in + xm_in + xp_in + ch + ends
-            k_ = str(k)
+            ym = jnp.where(lane < s, 0.0, b + pltpu.roll(b, s, 2))
+            yp = jnp.where(lane >= lanes - s, 0.0, b + pltpu.roll(b, lanes - s, 2))
+            xm = jnp.where(sub < s, 0.0, b + pltpu.roll(b, s, 1))
+            xp = jnp.where(sub >= SUB - s, 0.0, b + pltpu.roll(b, SUB - s, 1))
             put("cz" + k_, z, size, zm)
-            put("cym" + k_, z, size, ym_in)
-            put("cyp" + k_, z, size, yp_in)
-            put("cxm" + k_, z, size, xm_in)
-            put("cxp" + k_, z, size, xp_in)
+            put("cym" + k_, z, size, ym)
+            put("cyp" + k_, z, size, yp)
+            put("cxm" + k_, z, size, xm)
+            put("cxp" + k_, z, size, xp)
+            put("d" + k_, z, size, zm + zp + ym + yp + xm + xp + jnp.where(ends_y, b, 0.0))
+
+        chunks(z_all, step)
+        m["cz" + k_][rows(z_all, 1), :] = 0.5 * m[name][rows(z_all, 1), :]
+
+    def finish_coefficients(k):
+        s = 1 << k
+        z_all = depth >> k
+        name, k_ = "b" + str(k), str(k)
+        cz, d, hz = m["cz" + k_], m["d" + k_], m["hz_" + name]
+        outer = jnp.logical_or(sub < s, sub >= SUB - s)
+        arrive(name)
+        lo, hi = 0.5 * hz[0], 0.5 * hz[1]
+        cz[rows(0, 1), :] = cz[rows(0, 1), :] + lo
+        cz[rows(z_all, 1), :] = cz[rows(z_all, 1), :] + hi
+        d[rows(0, 1), :] = d[rows(0, 1), :] + lo
+        d[rows(z_all - 1, 1), :] = d[rows(z_all - 1, 1), :] + hi
+
+        def step(z, size):
+            ch = jnp.where(outer, 0.5 * (get(name, z + 1, size) + edge_rows(name, z, size)), 0.0)
+            diag = get("d" + k_, z, size) + ch
             put("ch" + k_, z, size, ch)
             put("d" + k_, z, size, diag)
             put("w" + k_, z, size, RELAX_WEIGHT / diag)
 
         chunks(z_all, step)
-        last = 0.5 * m[name][rows(z_all, 1), :] + 0.5 * m[name][rows(z_all + 1, 1), :]
-        m["cz" + str(k)][rows(z_all, 1), :] = last
 
     def inner_terms(k, name):
         s = 1 << k
@@ -307,13 +325,15 @@
         exchange("b" + str(k + 1), m["b" + str(k + 1)])
     gather("gb", 0.125 * restrict(get("b2", 1, depth >> 2), 2))
 
-    coefficients(0)
+    inner_coefficients(0)
     loads[2].wait()
     inner_terms(0, "vin")
+    finish_coefficients(0)
     relaxed(0, "vin", lambda z, size, value: put("v0", z + 1, size, value))
     exchange("v0", m["v0"])
     inner_terms(0, "v0")
-    coefficients(1)
+    inner_coefficients(1)
+    finish_coefficients(1)
     bc = column("gb")
     side("bc", bc)
 
@@ -335,7 +355,8 @@
     down(0, "v0")
     exchange("v1", m["v1"])
     inner_terms(1, "v1")
-    coefficients(2)
+    inner_coefficients(2)
+    finish_coefficients(2)
     down(1, "v1")
     exchange("v2", m["v2"])
     inner_terms(2, "v2")
@@ -355,7 +376,7 @@
         return jnp.where(lane_c >= NARROW - 8, pltpu.roll(v, NARROW - 9, 1), pltpu.roll(v, NARROW - 8, 1))
 
     arrive("bc")
-    b = {o: 0.5 * (bc if o == 0 else m["hx_bc"][far + o]) for o in range(-far, far + 1)}
+    b = {o: 0.5 * (bc if o == 0 else side_column("bc", o)) for o in range(-far, far + 1)}
     xp = {o: b[o] + b[o + 1] for o in range(-far, far)}
     ym, yp, zm, zp, diag, weight, inside = {}, {}, {}, {}, {}, {}, {}
     for o in range(-reach, reach + 1):
@@ -378,7 +399,7 @@
     own_forcing = column("gf")
     side("fc", own_forcing)
     arrive("fc")
-    forcing = {o: own_forcing if o == 0 else m["hx_fc"][reach + o] for o in range(-reach, reach + 1)}
+    forcing = {o: own_forcing if o == 0 else side_column("fc", o) for o in range(-reach, reach + 1)}
     guess = {o: weight[o] * forcing[o] for o in forcing}
 
     def total_of(o):

time: 55.7 us -> 54.6 us (0.980)
  Pallas kernels: 53.8 us -> 52.6 us
    pallas_call x1, Pallas kernels: 53.8 us -> 52.6 us  [local(): call(flat(source), flat(density), flat(pressure))]
where the time goes in v4:
time: 54.6 us; the launch traced here: 54.3 us
  Pallas kernels  52.6 us (96%)
  local copies, waits for them, and re-layouts  1.67 us (3%)
    pallas_call x1, Pallas kernels, local(): call(flat(source), flat(density), flat(pressure))  52.6 us
    unnamed x1, local copies, waits for them, and re-layouts  1.67 us

profile of v4, /device:TPU:7, one launch (start us, length us, event | category | flops | bytes accessed | tf_op | source)
XLA Modules:
  0.0 54.3 jit_solution(17218447005679012026)
XLA Ops:
  0.0 52.6 %v_cycle.1 = f32[128,512]{1,0:T(8,128)} custom-call(f32[128,512]{1,0:T(8,128)} %bitcast.5, f32[128,512]{1,0:T(8,128)} %bitcast.6, f32[128,512]{1,0:T(8,128)} %bitcast.7), custom_call_target="tpu_custom_call" | custom-call | tf_op jit(solution)/shard_map/v_cycle/pallas_call | solution.py:475
  52.6 1.7 %copy.5 = f32[16,8,512]{2,1,0:T(8,128)} copy(f32[16,8,512]{2,1,0:T(8,128)} %bitcast.4) | data formatting | bytes 524288

commit v5 on v4

--- a/solution.py
+++ b/solution.py
@@ -11,12 +11,13 @@
 RELAX_WEIGHT = 0.8
 KEEP = 1.0 - RELAX_WEIGHT
 MESH = pl.DeviceIdType.MESH
-CHUNK = 4
+CHUNK = 8
 SUB = 8
 NARROW = 128
-
-EXCHANGES = ("vin", "b0", "b1", "b2", "v0", "v1", "v2", "u2", "u1", "u0")
-LEVEL_OF = {"vin": 0, "b0": 0, "b1": 1, "b2": 2, "v0": 0, "v1": 1, "v2": 2, "u2": 2, "u1": 1, "u0": 0}
+GRANT = 56170000
+
+EXCHANGES = ("vin", "b0", "b1", "b2", "v0", "v1", "v2", "u2", "r2", "r1")
+LEVEL_OF = {"vin": 0, "b0": 0, "b1": 1, "b2": 2, "v0": 0, "v1": 1, "v2": 2, "u2": 2, "u1": 1, "u0": 0, "r2": 2, "r1": 1}
 SIDES = {"bc": COARSE_SWEEPS + 2, "fc": COARSE_SWEEPS + 1}
 GATHERS = ("gb", "gf")
 
@@ -44,8 +45,8 @@
     for name in GATHERS:
         plan["all_" + name] = pltpu.VMEM((peers * SUB, NARROW), jnp.float32)
         plan["own_" + name] = pltpu.VMEM((SUB, NARROW), jnp.float32)
-    plan["r2"] = field(depth >> 2)
-    plan["r1"] = field(depth >> 1)
+    plan["r2"] = field((depth >> 2) + 2)
+    plan["r1"] = field((depth >> 1) + 2)
     plan["col"] = pltpu.VMEM((3, column + 2 * SUB, NARROW), jnp.float32)
     plan["pick"] = pltpu.VMEM((SUB, NARROW), jnp.float32)
     plan["wide"] = pltpu.VMEM((SUB, lanes), jnp.float32)
@@ -218,12 +219,15 @@
             other = jnp.where((sub & s) != 0, other, pltpu.roll(value, SUB - s, 1))
         return value + other
 
-    def edge_rows(name, z, size):
+    def edge_rows(name, z, size, coarse=None):
         hx = m["hx_" + name]
         result = []
         for j in range(size):
-            lo = jnp.broadcast_to(hx[0, pl.ds(z + j, 1), :], (SUB, lanes))
-            hi = jnp.broadcast_to(hx[1, pl.ds(z + j, 1), :], (SUB, lanes))
+            lo, hi = hx[0, pl.ds(z + j, 1), :], hx[1, pl.ds(z + j, 1), :]
+            if coarse is not None:
+                below_it = pl.ds(z // 2 + j // 2, 1)
+                lo, hi = lo + m["hx_" + coarse][0, below_it, :], hi + m["hx_" + coarse][1, below_it, :]
+            lo, hi = jnp.broadcast_to(lo, (SUB, lanes)), jnp.broadcast_to(hi, (SUB, lanes))
             result.append(jnp.where(sub < SUB // 2, lo, hi))
         return jnp.stack(result)
 
@@ -290,26 +294,31 @@
 
         chunks(depth >> k, step)
 
-    def with_halo(k, name, use):
+    def with_halo(k, name, use, coarse=None):
         z_all = depth >> k
         k_ = str(k)
         t, cz, hz = m["t" + k_], m["cz" + k_], m["hz_" + name]
         arrive(name)
-        t[rows(0, 1), :] = t[rows(0, 1), :] + cz[rows(0, 1), :] * hz[0]
-        t[rows(z_all - 1, 1), :] = t[rows(z_all - 1, 1), :] + cz[rows(z_all, 1), :] * hz[1]
+        if coarse is None:
+            lo, hi = hz[0], hz[1]
+        else:
+            arrive(coarse)
+            lo, hi = hz[0] + m["hz_" + coarse][0], hz[1] + m["hz_" + coarse][1]
+        t[rows(0, 1), :] = t[rows(0, 1), :] + cz[rows(0, 1), :] * lo
+        t[rows(z_all - 1, 1), :] = t[rows(z_all - 1, 1), :] + cz[rows(z_all, 1), :] * hi
 
         def step(z, size):
-            use(z, size, get("t" + k_, z, size) + get("ch" + k_, z, size) * edge_rows(name, z, size))
+            use(z, size, get("t" + k_, z, size) + get("ch" + k_, z, size) * edge_rows(name, z, size, coarse))
 
         chunks(z_all, step)
 
-    def relaxed(k, name, store):
+    def relaxed(k, name, store, halo=None, coarse=None):
         k_ = str(k)
 
         def use(z, size, total):
             store(z, size, KEEP * get(name, z + 1, size) + get("w" + k_, z, size) * total)
 
-        with_halo(k, name, use)
+        with_halo(k, halo or name, use, coarse)
 
     loads[0].wait()
     loads[1].wait()
@@ -429,32 +438,32 @@
     m["hz_u2"][0] = m["hz_v2"][0] + spread(under(0))
     m["hz_u2"][1] = m["hz_v2"][1] + spread(under(3))
     inner_terms(2, "u2")
-    relaxed(2, "u2", lambda z, size, value: put("r2", z, size, value))
+    relaxed(2, "u2", lambda z, size, value: put("r2", z + 1, size, value))
+    exchange("r2", m["r2"])
 
     def add_coarse(k):
         fine, coarse, result = "v" + str(k), "r" + str(k + 1), "u" + str(k)
 
         def step(z, size):
             half = z // 2
-            c = get(coarse, half, size // 2)
+            c = get(coarse, half + 1, size // 2)
             c = jnp.stack([c[i // 2] for i in range(size)])
             put(result, z + 1, size, get(fine, z + 1, size) + c)
 
         chunks(depth >> k, step)
 
     add_coarse(1)
-    exchange("u1", m["u1"])
     inner_terms(1, "u1")
-    relaxed(1, "u1", lambda z, size, value: put("r1", z, size, value))
+    relaxed(1, "u1", lambda z, size, value: put("r1", z + 1, size, value), "v1", "r2")
+    exchange("r1", m["r1"])
 
     add_coarse(0)
-    exchange("u0", m["u0"])
     inner_terms(0, "u0")
 
     def store(z, size, value):
         out[rows(z, size), :] = value.reshape(size * SUB, lanes)
 
-    relaxed(0, "u0", store)
+    relaxed(0, "u0", store, "v0", "r1")
     for copy, sends in started:
         only(sends, lambda copy=copy: copy.wait_send())
 
@@ -469,7 +478,7 @@
         in_specs=[pl.BlockSpec(memory_space=pl.ANY)] * 3,
         out_specs=pl.BlockSpec(memory_space=pltpu.VMEM),
         scratch_shapes=list(plan.values()),
-        compiler_params=pltpu.CompilerParams(collective_id=0, has_side_effects=True),
+        compiler_params=pltpu.CompilerParams(collective_id=0, has_side_effects=True, vmem_limit_bytes=GRANT),
         name="v_cycle",
     )
     return call(flat(source), flat(density), flat(pressure)).reshape(depth, width, lanes)

time: 54.6 us -> 52.7 us (0.965)
  local copies, waits for them, and re-layouts: 1.67 us -> 0.71 us
  Pallas kernels: 52.6 us -> 51.9 us
    unnamed x1, local copies, waits for them, and re-layouts: 1.67 us -> 0.71 us
    pallas_call x1, Pallas kernels: 52.6 us -> 51.9 us  [local(): call(flat(source), flat(density), flat(pressure))]
where the time goes in v5:
time: 52.7 us; the launch traced here: 52.6 us
  Pallas kernels  51.9 us (98%)
  local copies, waits for them, and re-layouts  0.71 us (1%)
    pallas_call x1, Pallas kernels, local(): call(flat(source), flat(density), flat(pressure))  51.9 us

profile of v5, /device:TPU:7, one launch (start us, length us, event | category | flops | bytes accessed | tf_op | source)
XLA Modules:
  0.0 52.6 jit_solution(310894327618291879)
XLA Ops:
  0.0 51.9 %v_cycle.1 = f32[128,512]{1,0:T(8,128)S(1)} custom-call(f32[128,512]{1,0:T(8,128)} %bitcast.5, f32[128,512]{1,0:T(8,128)} %bitcast.6, f32[128,512]{1,0:T(8,128)} %bitcast.7), custom_call_target="tpu_custom_call" | custom-call | tf_op jit(solution)/shard_map/v_cycle/pallas_call | solution.py:484
  51.9 0.7 %copy.5 = f32[16,8,512]{2,1,0:T(8,128)} copy(f32[16,8,512]{2,1,0:T(8,128)S(1)} %bitcast.4) | data formatting | bytes 524288

commit v6 on v5

--- a/solution.py
+++ b/solution.py
@@ -11,7 +11,7 @@
 RELAX_WEIGHT = 0.8
 KEEP = 1.0 - RELAX_WEIGHT
 MESH = pl.DeviceIdType.MESH
-CHUNK = 8
+CHUNK = 16
 SUB = 8
 NARROW = 128
 GRANT = 56170000

time: 52.7 us -> 52.8 us (level)
  no operation moved by 1% of the time
where the time goes in v6:
time: 52.8 us; the launch traced here: 52.7 us
  Pallas kernels  51.9 us (98%)
  local copies, waits for them, and re-layouts  0.71 us (1%)
    pallas_call x1, Pallas kernels, local(): call(flat(source), flat(density), flat(pressure))  51.9 us

profile of v6, /device:TPU:7, one launch (start us, length us, event | category | flops | bytes accessed | tf_op | source)
XLA Modules:
  0.0 52.7 jit_solution(8531396514268239902)
XLA Ops:
  0.0 51.9 %v_cycle.1 = f32[128,512]{1,0:T(8,128)S(1)} custom-call(f32[128,512]{1,0:T(8,128)} %bitcast.5, f32[128,512]{1,0:T(8,128)} %bitcast.6, f32[128,512]{1,0:T(8,128)} %bitcast.7), custom_call_target="tpu_custom_call" | custom-call | tf_op jit(solution)/shard_map/v_cycle/pallas_call | solution.py:484
  52.0 0.7 %copy.5 = f32[16,8,512]{2,1,0:T(8,128)} copy(f32[16,8,512]{2,1,0:T(8,128)S(1)} %bitcast.4) | data formatting | bytes 524288
